TPU v7x, 128 devices: a whole 4x4x4 slice. The times are simulated.
128 devices in a mesh: req: 4 (over y), tile: 32 (over x, z, core).
Axes of the slice: x: 4, y: 4, z: 4, core: 2. Of those that a mesh axis runs over, the one named last changes fastest.
Arguments:
- image: bfloat16 [8, 4096, 2432], P('req', 'tile'), may hold values from -40 to 40
- text: bfloat16 [8, 154, 2432], P('req'), may hold values from -40 to 40
- pooled: float32 [8, 2432], P('req'), may hold values from -6 to 6
- timesteps: int32 [8], P('req'), may hold values from 0 to 999
- lengths: int32 [8], P('req'), may hold values from 1 to 4096, 16384 in all
- w_time: bfloat16 [256, 2432], replicated, may hold values from -0.375 to 0.375
- w_mod: bfloat16 [2432, 9728], P(None, 'tile'), may hold values from -0.125 to 0.125
- w_img: bfloat16 [2432, 6144], P(None, ('req', 'tile')), may hold values from -0.125 to 0.125
- w_txt: bfloat16 [2432, 6144], P(None, 'tile'), may hold values from -0.125 to 0.125
- q_gain: float32 [64], replicated, may hold values from 1 to 2.5
- k_gain: float32 [64], replicated, may hold values from 1 to 2.5
- text_q_gain: float32 [64], replicated, may hold values from 1 to 2.5
- text_k_gain: float32 [64], replicated, may hold values from 1 to 2.5
Outputs:
- image_attention: bfloat16 [8, 4096, 2048], P('req', 'tile')
- text_attention: bfloat16 [8, 154, 2048], P('req', None, 'tile')
Inputs may be any that keep to these rules, and one draw needn't show every extreme that they name: `lengths`: the image token counts of all 8 requests sum to 16384, and the largest is exactly 4096.
All inputs are finite; a program needn't handle non-finite values. No bound on the sum of `lengths` on one device may be relied on, other than what follows from the above.
Results may differ from a plain program's by a relative error of at most 0.02.
Values may be sent and summed in bfloat16 or wider, within the bound.
A program may use at most 128 MiB of HBM per device.

v0:
```python
import math

import jax
import jax.numpy as jnp
from jax import lax
from jax.sharding import PartitionSpec as P

epsilon = 1e-06


def time_features(step_index, feature_count):
    half_count = feature_count // 2
    frequency = jnp.exp(-math.log(10000.0) * jnp.arange(half_count, dtype=jnp.float32) / half_count)
    angles = step_index.astype(jnp.float32)[:, None] * frequency[None, :]
    return jnp.concatenate([jnp.cos(angles), jnp.sin(angles)], axis=-1).astype(jnp.bfloat16)


def modulate(tokens, shift, scale):
    values = tokens.astype(jnp.float32)
    center = jnp.mean(values, axis=-1, keepdims=True)
    spread = jnp.mean(jnp.square(values - center), axis=-1, keepdims=True)
    normed = (values - center) * lax.rsqrt(spread + epsilon)
    return (normed * (1.0 + scale.astype(jnp.float32)) + shift.astype(jnp.float32)).astype(
        jnp.bfloat16
    )


def rms_gain(vectors, gain):
    factor = lax.rsqrt(jnp.mean(jnp.square(vectors), axis=-1, keepdims=True) + epsilon)
    return (vectors * factor * gain).astype(jnp.bfloat16)


def pack_heads(qkv, head_dim, q_gain, k_gain):
    lead = qkv.shape[:2]
    head_count = qkv.shape[-1] // (3 * head_dim)
    qkv = qkv.reshape(lead + (head_count, 3, head_dim))
    return jnp.concatenate(
        [
            rms_gain(qkv[:, :, :, 0:1, :], q_gain),
            rms_gain(qkv[:, :, :, 1:2, :], k_gain),
            qkv[:, :, :, 2:3, :].astype(jnp.bfloat16),
        ],
        axis=3,
    ).reshape(lead + (head_count, 3 * head_dim))


def local(
    image,
    text,
    pooled,
    timesteps,
    lengths,
    w_time,
    w_mod,
    w_img,
    w_txt,
    q_gain,
    k_gain,
    text_q_gain,
    text_k_gain,
):
    tile_count = lax.axis_size("tile")
    group_count, local_rows, model_width = image.shape
    seq_len = local_rows * tile_count
    text_len = text.shape[1]
    head_dim = q_gain.shape[0]
    heads_here = w_txt.shape[1] // (3 * head_dim)
    score_scale = head_dim ** (-0.5)
    block = min(512, seq_len)
    features = time_features(timesteps, w_time.shape[0])
    cond_act = jax.nn.silu(
        pooled + jnp.dot(features, w_time, preferred_element_type=jnp.float32)
    ).astype(jnp.bfloat16)
    mod_part = jnp.dot(cond_act, w_mod, preferred_element_type=jnp.float32).astype(jnp.bfloat16)
    modulation = lax.all_gather(mod_part, "tile", axis=1, tiled=True)
    h_img = modulate(
        image,
        modulation[:, None, 0:model_width],
        modulation[:, None, model_width : 2 * model_width],
    )
    qkv_img = jnp.einsum(
        "gpd,dc->gpc",
        h_img,
        lax.all_gather(w_img, ("req", "tile"), axis=1, tiled=True),
        preferred_element_type=jnp.float32,
    )
    packed = pack_heads(qkv_img, head_dim, q_gain, k_gain)
    by_head = lax.all_to_all(packed, "tile", split_axis=2, concat_axis=1, tiled=True)
    by_head = by_head.reshape(group_count, seq_len, heads_here, 3, head_dim)
    h_txt = modulate(
        text,
        modulation[:, None, 2 * model_width : 3 * model_width],
        modulation[:, None, 3 * model_width : 4 * model_width],
    )
    qkv_txt = jnp.einsum("gtd,dc->gtc", h_txt, w_txt, preferred_element_type=jnp.float32).reshape(
        group_count, text_len, heads_here, 3, head_dim
    )
    text_queries = jnp.moveaxis(rms_gain(qkv_txt[:, :, :, 0, :], text_q_gain), 2, 1)
    text_keys = jnp.moveaxis(rms_gain(qkv_txt[:, :, :, 1, :], text_k_gain), 2, 1)
    text_values = jnp.moveaxis(qkv_txt[:, :, :, 2, :].astype(jnp.bfloat16), 2, 1)
    image_queries = jnp.moveaxis(by_head[:, :, :, 0, :], 2, 1)
    image_keys = jnp.moveaxis(by_head[:, :, :, 1, :], 2, 1)
    image_values = jnp.moveaxis(by_head[:, :, :, 2, :], 2, 1)
    slot_live = (jnp.arange(seq_len, dtype=jnp.int32)[None, :] < lengths[:, None]).astype(
        jnp.float32
    )
    keys = jnp.concatenate([text_keys, image_keys], axis=2)
    values = jnp.concatenate([text_values, image_values], axis=2)
    key_mask = jnp.concatenate([jnp.ones((group_count, text_len), jnp.float32), slot_live], axis=1)

    def attend_block(query_block):
        scores = (
            jnp.einsum("ghqe,ghke->ghqk", query_block, keys, preferred_element_type=jnp.float32)
            * score_scale
        )
        weights = jnp.exp(scores) * key_mask[:, None, None, :]
        total = jnp.sum(weights, axis=-1)
        summed = jnp.einsum(
            "ghqk,ghke->ghqe",
            weights.astype(jnp.bfloat16),
            values,
            preferred_element_type=jnp.float32,
        )
        return summed / total[..., None]

    text_result = attend_block(text_queries)
    block_count = seq_len // block
    query_blocks = jnp.moveaxis(
        image_queries.reshape(group_count, heads_here, block_count, block, head_dim), 2, 0
    )
    image_result = lax.map(attend_block, query_blocks)
    image_result = jnp.moveaxis(image_result, 0, 2).reshape(
        group_count, heads_here, seq_len, head_dim
    )
    image_result = image_result * slot_live[:, None, :, None]
    image_heads = (
        jnp.moveaxis(image_result, 1, 2)
        .reshape(group_count, seq_len, heads_here * head_dim)
        .astype(jnp.bfloat16)
    )
    image_attention = lax.all_to_all(image_heads, "tile", split_axis=1, concat_axis=2, tiled=True)
    text_attention = (
        jnp.moveaxis(text_result, 1, 2)
        .reshape(group_count, text_len, heads_here * head_dim)
        .astype(jnp.bfloat16)
    )
    return (image_attention, text_attention)


def solution(mesh):
    in_specs = (
        P("req", "tile", None),
        P("req", None, None),
        P("req", None),
        P("req"),
        P("req"),
        P(),
        P(None, "tile"),
        P(None, ("req", "tile")),
        P(None, "tile"),
        P(),
        P(),
        P(),
        P(),
    )
    out_specs = (P("req", "tile", None), P("req", None, "tile"))
    return jax.shard_map(local, mesh=mesh, in_specs=in_specs, out_specs=out_specs, check_vma=False)
```

profile of v0, /device:TPU:25, one launch (start us, length us, event | category | flops | bytes accessed | tf_op | source)
XLA Modules:
  0.0 316.6 jit_solution(9887825131999593207)
XLA Ops:
  10.7 26.1 %all-gather = bf16[32,304,2]{1,2,0:T(2,128)(2,1)S(1)} all-gather(bf16[1,304,2]{1,2,0:T(2,128)(2,1)S(1)} %fusion.59), channel_id=1, replica_groups=mesh['req'=4,'tile'=32] {'tile'}, dimensions={0}, use_global_device_ids=true | all-gather | bytes 40128 | tf_op jit(solution)/shard_map/all_gather | solution.py:75
  41.8 72.4 %all-gather.3.cloned.1.call-done = bf16[2432,6144]{0,1:T(8,128)(2,1)} async-done(((bf16[2432,48]{0,1:T(8,128)(2,1)}), bf16[2432,6144]{0,1:T(8,128)(2,1)}) %all-gather.3.cloned.1.call-update) | async-done | bytes 29884432 | tf_op jit(solution)/shard_map/all_gather | solution.py:84
  114.2 13.6 %fusion.26 = f32[2,128,6144]{1,2,0:T(8,128)S(1)} fusion(bf16[2432,6144]{0,1:T(8,128)(2,1)} %all-gather.3.cloned.1.call-done, bf16[2,128,2432]{2,1,0:T(8,128)(2,1)S(1)} %copy-done.3, f32[2,2432]{1,0:T(2,128)S(1)} %get-tuple-element.69, f32[2,2432]{1,0:T(2,128)S(1)} %get-tuple-element.67, f32[2,128]{1,0:T(2,128)S(1)} %add_rsqrt_fusion.5, ...), kind=kOutput, calls=%fused_computation.14 | convolution fusion | flops 7654146048 | bytes 37462016 | tf_op jit(solution)/shard_map/gpd,dc->gpc/dot_general | solution.py:81
  132.0 5.4 %all-to-all-start = ((bf16[2,128,32,192]{1,3,0,2:T(8,128)(2,1)}), bf16[2,128,32,192]{1,3,0,2:T(8,128)(2,1)}, u32[]{:S(2)}, u32[]{:S(2)}) async-start(bf16[2,128,32,192]{1,3,0,2:T(8,128)(2,1)} %copy.78), calls=%async_computation | async-start | bytes 6291456 | tf_op jit(solution)/shard_map/all_to_all | solution.py:88
  143.5 33.8 %all-to-all-done = bf16[2,128,32,192]{1,3,0,2:T(8,128)(2,1)} async-done(((bf16[2,128,32,192]{1,3,0,2:T(8,128)(2,1)}), bf16[2,128,32,192]{1,3,0,2:T(8,128)(2,1)}, u32[]{:S(2)}, u32[]{:S(2)}) %all-to-all-start) | async-done | bytes 3145760 | tf_op jit(solution)/shard_map/all_to_all | solution.py:88
  177.2 5.6 %copy.79 = bf16[2,32,128,1,192]{2,1,4,0,3:T(8,128)(2,1)} copy(bf16[2,32,128,1,192]{2,4,0,1,3:T(8,128)(2,1)} %bitcast.11) | data formatting | bytes 6291456 | tf_op jit(solution)/shard_map/all_to_all | solution.py:88
  182.8 5.8 %reshape.273 = bf16[2,4096,1,3,64]{1,4,3,0,2:T(8,128)(2,1)} reshape(bf16[2,32,128,1,192]{2,1,4,0,3:T(8,128)(2,1)} %copy.79) | data formatting | bytes 6291456 | tf_op jit(solution)/shard_map/reshape | solution.py:89
  193.3 67.5 %while.10 = (s32[]{:T(128)}, f32[8,2,1,512,64]{3,4,1,2,0:T(8,128)}, bf16[8,2,1,512,64]{3,4,1,2,0:T(8,128)(2,1)}, bf16[2,1,4250,64]{2,3,0,1:T(8,128)(2,1)S(1)}, f...) while((s32[]{:T(128)}, f32[8,2,1,512,64]{3,4,1,2,0:T(8,128)}, ...), condition=%wide.region_9.10_spmd, body=%wide.region_7.0_spmd.sunk | while | flops 1140288512 | bytes 37462508 | solution.py:131
  193.3 4.8 %fusion.93 = (f32[2,512]{1,0:T(2,128)S(1)}, f32[2,512,4250]{1,2,0:T(8,128)S(1)}) fusion(f32[2,4250]{1,0:T(2,128)S(1)} %get-tuple-element.137, bf16[2,1,4250,64]{2,3,0,1:T(8,128)(2,1)S(1)} %get-tuple-element.136, bf16[8,2,1,512,64]{3,4,1,2,0:T(8,128)(2,1)} %get-tuple-element.135, s32[]{:T(128)} %get-tuple-element.126), kind=kOutput, calls=%fused_computation.1.clone.1 | convolution fusion | flops 570110976 | bytes 18665680 | tf_op jit(solution)/shard_map/while/body/eval_jaxpr/ghqe,ghke->ghqk/dot_general | solution.py:113
  201.8 4.8 %fusion.93 = (f32[2,512]{1,0:T(2,128)S(1)}, f32[2,512,4250]{1,2,0:T(8,128)S(1)}) fusion(f32[2,4250]{1,0:T(2,128)S(1)} %get-tuple-element.137, bf16[2,1,4250,64]{2,3,0,1:T(8,128)(2,1)S(1)} %get-tuple-element.136, bf16[8,2,1,512,64]{3,4,1,2,0:T(8,128)(2,1)} %get-tuple-element.135, s32[]{:T(128)} %get-tuple-element.126), kind=kOutput, calls=%fused_computation.1.clone.1 | convolution fusion | flops 570110976 | bytes 18665680 | tf_op jit(solution)/shard_map/while/body/eval_jaxpr/ghqe,ghke->ghqk/dot_general | solution.py:113
  210.2 4.8 %fusion.93 = (f32[2,512]{1,0:T(2,128)S(1)}, f32[2,512,4250]{1,2,0:T(8,128)S(1)}) fusion(f32[2,4250]{1,0:T(2,128)S(1)} %get-tuple-element.137, bf16[2,1,4250,64]{2,3,0,1:T(8,128)(2,1)S(1)} %get-tuple-element.136, bf16[8,2,1,512,64]{3,4,1,2,0:T(8,128)(2,1)} %get-tuple-element.135, s32[]{:T(128)} %get-tuple-element.126), kind=kOutput, calls=%fused_computation.1.clone.1 | convolution fusion | flops 570110976 | bytes 18665680 | tf_op jit(solution)/shard_map/while/body/eval_jaxpr/ghqe,ghke->ghqk/dot_general | solution.py:113
  215.0 3.6 %fusion.94 = f32[8,2,1,512,64]{3,4,1,2,0:T(8,128)} fusion(f32[8,2,1,512,64]{3,4,1,2,0:T(8,128)} %get-tuple-element.127, s32[]{:T(128)} %get-tuple-element.126, bf16[2,1,4250,64]{2,3,0,1:T(8,128)(2,1)S(1)} %get-tuple-element.138, f32[2,512,4250]{1,2,0:T(8,128)S(1)} %get-tuple-element.117, f32[2,4250]{1,0:T(2,128)S(1)} %get-tuple-element.137, ...), kind=kOutput, calls=%fused_computation.9.clone.1 | convolution fusion | flops 570177536 | bytes 18796752 | tf_op jit(solution)/shard_map/while/body/eval_jaxpr/ghqk,ghke->ghqe/dot_general | solution.py:118
  218.6 4.8 %fusion.93 = (f32[2,512]{1,0:T(2,128)S(1)}, f32[2,512,4250]{1,2,0:T(8,128)S(1)}) fusion(f32[2,4250]{1,0:T(2,128)S(1)} %get-tuple-element.137, bf16[2,1,4250,64]{2,3,0,1:T(8,128)(2,1)S(1)} %get-tuple-element.136, bf16[8,2,1,512,64]{3,4,1,2,0:T(8,128)(2,1)} %get-tuple-element.135, s32[]{:T(128)} %get-tuple-element.126), kind=kOutput, calls=%fused_computation.1.clone.1 | convolution fusion | flops 570110976 | bytes 18665680 | tf_op jit(solution)/shard_map/while/body/eval_jaxpr/ghqe,ghke->ghqk/dot_general | solution.py:113
  227.1 4.8 %fusion.93 = (f32[2,512]{1,0:T(2,128)S(1)}, f32[2,512,4250]{1,2,0:T(8,128)S(1)}) fusion(f32[2,4250]{1,0:T(2,128)S(1)} %get-tuple-element.137, bf16[2,1,4250,64]{2,3,0,1:T(8,128)(2,1)S(1)} %get-tuple-element.136, bf16[8,2,1,512,64]{3,4,1,2,0:T(8,128)(2,1)} %get-tuple-element.135, s32[]{:T(128)} %get-tuple-element.126), kind=kOutput, calls=%fused_computation.1.clone.1 | convolution fusion | flops 570110976 | bytes 18665680 | tf_op jit(solution)/shard_map/while/body/eval_jaxpr/ghqe,ghke->ghqk/dot_general | solution.py:113
  235.5 4.8 %fusion.93 = (f32[2,512]{1,0:T(2,128)S(1)}, f32[2,512,4250]{1,2,0:T(8,128)S(1)}) fusion(f32[2,4250]{1,0:T(2,128)S(1)} %get-tuple-element.137, bf16[2,1,4250,64]{2,3,0,1:T(8,128)(2,1)S(1)} %get-tuple-element.136, bf16[8,2,1,512,64]{3,4,1,2,0:T(8,128)(2,1)} %get-tuple-element.135, s32[]{:T(128)} %get-tuple-element.126), kind=kOutput, calls=%fused_computation.1.clone.1 | convolution fusion | flops 570110976 | bytes 18665680 | tf_op jit(solution)/shard_map/while/body/eval_jaxpr/ghqe,ghke->ghqk/dot_general | solution.py:113
  243.9 4.8 %fusion.93 = (f32[2,512]{1,0:T(2,128)S(1)}, f32[2,512,4250]{1,2,0:T(8,128)S(1)}) fusion(f32[2,4250]{1,0:T(2,128)S(1)} %get-tuple-element.137, bf16[2,1,4250,64]{2,3,0,1:T(8,128)(2,1)S(1)} %get-tuple-element.136, bf16[8,2,1,512,64]{3,4,1,2,0:T(8,128)(2,1)} %get-tuple-element.135, s32[]{:T(128)} %get-tuple-element.126), kind=kOutput, calls=%fused_computation.1.clone.1 | convolution fusion | flops 570110976 | bytes 18665680 | tf_op jit(solution)/shard_map/while/body/eval_jaxpr/ghqe,ghke->ghqk/dot_general | solution.py:113
  248.7 3.6 %fusion.94 = f32[8,2,1,512,64]{3,4,1,2,0:T(8,128)} fusion(f32[8,2,1,512,64]{3,4,1,2,0:T(8,128)} %get-tuple-element.127, s32[]{:T(128)} %get-tuple-element.126, bf16[2,1,4250,64]{2,3,0,1:T(8,128)(2,1)S(1)} %get-tuple-element.138, f32[2,512,4250]{1,2,0:T(8,128)S(1)} %get-tuple-element.117, f32[2,4250]{1,0:T(2,128)S(1)} %get-tuple-element.137, ...), kind=kOutput, calls=%fused_computation.9.clone.1 | convolution fusion | flops 570177536 | bytes 18796752 | tf_op jit(solution)/shard_map/while/body/eval_jaxpr/ghqk,ghke->ghqe/dot_general | solution.py:118
  252.4 4.8 %fusion.93 = (f32[2,512]{1,0:T(2,128)S(1)}, f32[2,512,4250]{1,2,0:T(8,128)S(1)}) fusion(f32[2,4250]{1,0:T(2,128)S(1)} %get-tuple-element.137, bf16[2,1,4250,64]{2,3,0,1:T(8,128)(2,1)S(1)} %get-tuple-element.136, bf16[8,2,1,512,64]{3,4,1,2,0:T(8,128)(2,1)} %get-tuple-element.135, s32[]{:T(128)} %get-tuple-element.126), kind=kOutput, calls=%fused_computation.1.clone.1 | convolution fusion | flops 570110976 | bytes 18665680 | tf_op jit(solution)/shard_map/while/body/eval_jaxpr/ghqe,ghke->ghqk/dot_general | solution.py:113
  260.8 4.1 %copy.91 = f32[2,1,8,512,64]{3,2,4,0,1:T(8,128)} copy(f32[2,1,8,512,64]{3,4,0,1,2:T(8,128)} %bitcast.19) | data formatting | bytes 4194304 | tf_op jit(solution)/shard_map/transpose | solution.py:132
  269.4 3.9 %copy.92 = bf16[2,4096,64]{2,0,1:T(2,128)(2,1)} copy(bf16[2,4096,64]{1,2,0:T(8,128)(2,1)S(1)} %multiply_convert_fusion) | data formatting | bytes 2097152 | tf_op jit(solution)/shard_map/convert_element_type | solution.py:139
  273.3 5.9 %reshape.282 = bf16[32,2,8192]{2,1,0:T(2,128)(2,1)} reshape(bf16[4096,2,64]{2,1,0:T(2,128)(2,1)} %bitcast.116) | data formatting | bytes 2097152
  279.2 5.0 %all-to-all-start.1 = ((bf16[32,2,8192]{2,1,0:T(2,128)(2,1)}), bf16[32,2,8192]{2,1,0:T(2,128)(2,1)S(1)}, u32[]{:S(2)}, u32[]{:S(2)}) async-start(bf16[32,2,8192]{2,1,0:T(2,128)(2,1)} %reshape.282), calls=%async_computation.1 | async-start | bytes 2097152 | tf_op jit(solution)/shard_map/all_to_all | solution.py:141
  287.5 13.6 %all-to-all-done.1 = bf16[32,2,8192]{2,1,0:T(2,128)(2,1)S(1)} async-done(((bf16[32,2,8192]{2,1,0:T(2,128)(2,1)}), bf16[32,2,8192]{2,1,0:T(2,128)(2,1)S(1)}, u32[]{:S(2)}, u32[]{:S(2)}) %all-to-all-start.1) | async-done | bytes 1048608 | tf_op jit(solution)/shard_map/all_to_all | solution.py:141
  303.5 5.0 %copy.99 = bf16[2,32,128,64]{2,3,1,0:T(8,128)(2,1)S(1)} copy(bf16[2,32,128,64]{3,0,2,1:T(2,128)(2,1)} %bitcast.117) | data formatting | bytes 2097152 | tf_op jit(solution)/shard_map/all_to_all | solution.py:141
  (80 shorter events, 56.4 us)
Async XLA Ops:
  7.2 1.6 copy-start
  7.2 29.8 %copy-start.8 = (s32[2]{0:T(128)S(1)}, s32[2]{0:T(128)}, u32[]{:S(2)}) copy-start(s32[2]{0:T(128)} %param.19) | copy-start | bytes 28
  7.2 107.0 %all-gather.3.cloned.1.call-start = ((), (), s32[]{:S(2)}) async-start(), calls=%async_computation.2 | async-start | bytes 30117888 | tf_op jit(solution)/shard_map/all_gather | solution.py:84
  10.7 29.8 %copy-start.2 = (bf16[2,154,2432]{2,0,1:T(2,128)(2,1)S(1)}, bf16[2,154,2432]{2,0,1:T(2,128)(2,1)}, u32[]{:S(2)}) copy-start(bf16[2,154,2432]{2,0,1:T(2,128)(2,1)} %param.16) | copy-start | bytes 4494340
  36.8 77.4 %copy-start.3 = (bf16[2,128,2432]{2,1,0:T(8,128)(2,1)S(1)}, bf16[2,128,2432]{2,1,0:T(8,128)(2,1)}, u32[]{:S(2)}) copy-start(bf16[2,128,2432]{2,1,0:T(8,128)(2,1)} %param.15) | copy-start | bytes 3735556
  127.8 1.0 copy-start.10
  127.8 1.0 copy-start.11
  132.0 45.2 %all-to-all-start = ((bf16[2,128,32,192]{1,3,0,2:T(8,128)(2,1)}), bf16[2,128,32,192]{1,3,0,2:T(8,128)(2,1)}, u32[]{:S(2)}, u32[]{:S(2)}) async-start(bf16[2,128,32,192]{1,3,0,2:T(8,128)(2,1)} %copy.78), calls=%async_computation | async-start | bytes 6291456 | tf_op jit(solution)/shard_map/all_to_all | solution.py:88
  137.5 5.1 %copy-start.12 = (bf16[2432,192]{0,1:T(8,128)(2,1)S(1)}, bf16[2432,192]{0,1:T(8,128)(2,1)}, u32[]{:S(2)}) copy-start(bf16[2432,192]{0,1:T(8,128)(2,1)} %param.23) | copy-start | bytes 2801668
  142.6 0.8 copy-start.9
  190.8 2.1 copy-start.6
  190.8 2.1 copy-start.4
  273.3 10.9 %copy-start.7 = (bf16[2,1,4096,64]{2,3,0,1:T(8,128)(2,1)S(1)}, bf16[2,1,4096,64]{2,3,0,1:T(8,128)(2,1)}, u32[]{:S(2)}) copy-start(bf16[2,1,4096,64]{2,3,0,1:T(8,128)(2,1)} %copy-done.6) | copy-start | bytes 3145732
  273.3 10.9 %copy-start.13 = (f32[64]{0:T(128)S(1)}, f32[64]{0:T(128)}, u32[]{:S(2)}) copy-start(f32[64]{0:T(128)} %param.26) | copy-start | bytes 772
  279.2 21.9 %all-to-all-start.1 = ((bf16[32,2,8192]{2,1,0:T(2,128)(2,1)}), bf16[32,2,8192]{2,1,0:T(2,128)(2,1)S(1)}, u32[]{:S(2)}, u32[]{:S(2)}) async-start(bf16[32,2,8192]{2,1,0:T(2,128)(2,1)} %reshape.282), calls=%async_computation.1 | async-start | bytes 2097152 | tf_op jit(solution)/shard_map/all_to_all | solution.py:141
  284.2 1.6 copy-start.5
  303.5 6.3 %copy-start.1 = (bf16[2432,304]{0,1:T(8,128)(2,1)S(1)}, bf16[2432,304]{0,1:T(8,128)(2,1)}, u32[]{:S(2)}) copy-start(bf16[2432,304]{0,1:T(8,128)(2,1)} %param.21) | copy-start | bytes 4435972
Sparse Core Ops, SparseCore 0:
  11.0 103.1 all-gather.2
where the time goes:
time: 320 us; the launch traced here: 317 us
  waiting for transfers between devices  120 us (38%)
  matrix products  86.9 us (27%)
  local copies, waits for them, and re-layouts  43 us (13%)
  blocking collectives  26.1 us (8%)
  other arithmetic  15.2 us (5%)
  between operations  14.4 us (4%)
  starting transfers between devices  10.4 us (3%)
    all_gather x1, waiting for transfers between devices, local(): lax.all_gather(w_img, ('req', 'tile'), axis=1, tiled=True)  72.4 us
    dot_general x9, matrix products, attend_block(): jnp.einsum('ghqe,ghke->ghqk', query_block, keys, preferred_element_type=j...  39.9 us
    all_to_all x1, waiting for transfers between devices, local(): lax.all_to_all(packed, 'tile', split_axis=2, concat_axis=1, tiled=True)  33.8 us
    dot_general x9, matrix products, attend_block(): jnp.einsum('ghqk,ghke->ghqe', weights.astype(jnp.bfloat16), values, prefe...  30.8 us
    all_gather x1, blocking collectives, local(): modulation = lax.all_gather(mod_part, 'tile', axis=1, tiled=True)  26.1 us
    dot_general x1, matrix products, local(): jnp.einsum('gpd,dc->gpc', h_img, lax.all_gather(w_img, ('req', 'tile'), a...  13.6 us
    all_to_all x1, waiting for transfers between devices, local(): lax.all_to_all(image_heads, 'tile', split_axis=1, concat_axis=2, tiled=True)  13.6 us
    unnamed x33, local copies, waits for them, and re-layouts  10.1 us
  transfers between devices with their start and end apart: 3, of which 3 were waited for; matrix products, arithmetic and copies ran while one was open for 5% of the time, Pallas kernels for 0%

commit v1 on v0

--- a/solution.py
+++ b/solution.py
@@ -1,8 +1,11 @@
+import functools
 import math
 
 import jax
 import jax.numpy as jnp
 from jax import lax
+from jax.experimental import pallas as pl
+from jax.experimental.pallas import tpu as pltpu
 from jax.sharding import PartitionSpec as P
 
 epsilon = 1e-06
@@ -30,18 +33,95 @@
     return (vectors * factor * gain).astype(jnp.bfloat16)
 
 
-def pack_heads(qkv, head_dim, q_gain, k_gain):
-    lead = qkv.shape[:2]
-    head_count = qkv.shape[-1] // (3 * head_dim)
-    qkv = qkv.reshape(lead + (head_count, 3, head_dim))
-    return jnp.concatenate(
-        [
-            rms_gain(qkv[:, :, :, 0:1, :], q_gain),
-            rms_gain(qkv[:, :, :, 1:2, :], k_gain),
-            qkv[:, :, :, 2:3, :].astype(jnp.bfloat16),
-        ],
-        axis=3,
-    ).reshape(lead + (head_count, 3 * head_dim))
+LANES = 128
+QUERY_BLOCK = 512
+KEY_BLOCK = 512
+
+
+def attend_kernel(lengths_ref, query_ref, key_ref, value_ref, text_key_ref, text_value_ref, out_ref, aug_ref, text_aug_ref, *, text_len, groups, width):
+    step = pl.program_id(0)
+    rows = query_ref.shape[0]
+    seq_len = key_ref.shape[0]
+
+    @pl.when(step == 0)
+    def _():
+        for group in range(groups):
+            text_lane = lax.broadcasted_iota(jnp.int32, text_value_ref.shape, 1) // width == group
+            text_live = lax.broadcasted_iota(jnp.int32, text_value_ref.shape, 0) < text_len
+            text_value = text_value_ref[...].astype(jnp.float32)
+            text_aug_ref[group] = jnp.where(
+                text_live, jnp.where(text_lane, text_value, 1.0), 0.0
+            ).astype(jnp.bfloat16)
+
+            def fill(index, carry):
+                start = pl.multiple_of(index * KEY_BLOCK, KEY_BLOCK)
+                shape = (KEY_BLOCK, LANES)
+                own = lax.broadcasted_iota(jnp.int32, shape, 1) // width == group
+                live = lax.broadcasted_iota(jnp.int32, shape, 0) + start < lengths_ref[group]
+                value = value_ref[pl.ds(start, KEY_BLOCK), :].astype(jnp.float32)
+                aug_ref[group, pl.ds(start, KEY_BLOCK), :] = jnp.where(
+                    live, jnp.where(own, value, 1.0), 0.0
+                ).astype(jnp.bfloat16)
+                return carry
+
+            lax.fori_loop(0, seq_len // KEY_BLOCK, fill, 0)
+
+    lane = lax.broadcasted_iota(jnp.int32, (rows, LANES), 1) // width
+    row = lax.broadcasted_iota(jnp.int32, (rows, LANES), 0) + step * rows
+    out_ref[...] = jnp.zeros_like(out_ref)
+    for group in range(groups):
+        length = lengths_ref[group]
+
+        @pl.when(step * rows < length)
+        def _():
+            query = jnp.where(lane == group, query_ref[...].astype(jnp.float32), 0.0).astype(
+                jnp.bfloat16
+            )
+
+            def part(keys, augmented):
+                scores = lax.dot_general(
+                    query, keys, (((1,), (1,)), ((), ())), preferred_element_type=jnp.float32
+                )
+                weights = jnp.exp2(scores).astype(jnp.bfloat16)
+                return jnp.dot(weights, augmented, preferred_element_type=jnp.float32)
+
+            def body(index, acc):
+                start = pl.multiple_of(index * KEY_BLOCK, KEY_BLOCK)
+                return acc + part(
+                    key_ref[pl.ds(start, KEY_BLOCK), :],
+                    aug_ref[group, pl.ds(start, KEY_BLOCK), :],
+                )
+
+            acc = part(text_key_ref[...], text_aug_ref[group])
+            acc = lax.fori_loop(0, (length + KEY_BLOCK - 1) // KEY_BLOCK, body, acc)
+            total = pltpu.roll(acc, LANES // 2, 1)
+            result = jnp.where(row < length, acc / total, 0.0).astype(jnp.bfloat16)
+            out_ref[...] = jnp.where(lane == group, result, out_ref[...])
+
+
+def attend_image(lengths, by_head, text_key, text_value, text_len, groups, width):
+    seq_len = by_head.shape[0]
+    text_rows = text_key.shape[0]
+    return pl.pallas_call(
+        functools.partial(attend_kernel, text_len=text_len, groups=groups, width=width),
+        grid_spec=pltpu.PrefetchScalarGridSpec(
+            num_scalar_prefetch=1,
+            grid=(seq_len // QUERY_BLOCK,),
+            in_specs=[
+                pl.BlockSpec((QUERY_BLOCK, LANES), lambda i, n: (i, 0)),
+                pl.BlockSpec((seq_len, LANES), lambda i, n: (0, 1)),
+                pl.BlockSpec((seq_len, LANES), lambda i, n: (0, 2)),
+                pl.BlockSpec((text_rows, LANES), lambda i, n: (0, 0)),
+                pl.BlockSpec((text_rows, LANES), lambda i, n: (0, 0)),
+            ],
+            out_specs=pl.BlockSpec((QUERY_BLOCK, LANES), lambda i, n: (i, 0)),
+            scratch_shapes=[
+                pltpu.VMEM((groups, seq_len, LANES), jnp.bfloat16),
+                pltpu.VMEM((groups, text_rows, LANES), jnp.bfloat16),
+            ],
+        ),
+        out_shape=jax.ShapeDtypeStruct((seq_len, LANES), jnp.bfloat16),
+    )(lengths, by_head, by_head, by_head, text_key, text_value)
 
 
 def local(
@@ -66,7 +146,19 @@
     head_dim = q_gain.shape[0]
     heads_here = w_txt.shape[1] // (3 * head_dim)
     score_scale = head_dim ** (-0.5)
-    block = min(512, seq_len)
+    same_core = [[t for t in range(tile_count) if t % 2 == c] for c in range(2)]
+    all_same_core = [
+        [r * tile_count + t for r in range(lax.axis_size("req")) for t in same_core[c]]
+        for c in range(2)
+    ]
+    turned = lax.ppermute(
+        w_img,
+        "tile",
+        [(t, t // 8 * 8 + ((t % 8) * 2 + (t % 8) // 4) % 8) for t in range(tile_count)],
+    )
+    w_half = lax.all_gather(
+        turned, ("req", "tile"), axis=1, tiled=True, axis_index_groups=all_same_core
+    )
     features = time_features(timesteps, w_time.shape[0])
     cond_act = jax.nn.silu(
         pooled + jnp.dot(features, w_time, preferred_element_type=jnp.float32)
@@ -78,15 +170,31 @@
         modulation[:, None, 0:model_width],
         modulation[:, None, model_width : 2 * model_width],
     )
-    qkv_img = jnp.einsum(
-        "gpd,dc->gpc",
-        h_img,
-        lax.all_gather(w_img, ("req", "tile"), axis=1, tiled=True),
-        preferred_element_type=jnp.float32,
-    )
-    packed = pack_heads(qkv_img, head_dim, q_gain, k_gain)
-    by_head = lax.all_to_all(packed, "tile", split_axis=2, concat_axis=1, tiled=True)
-    by_head = by_head.reshape(group_count, seq_len, heads_here, 3, head_dim)
+    core = lax.axis_index("tile") % 2
+    h_other = lax.ppermute(h_img, "tile", [(t, t ^ 1) for t in range(tile_count)])
+    h_pair = jnp.where(
+        core == 0,
+        jnp.concatenate([h_img, h_other], axis=1),
+        jnp.concatenate([h_other, h_img], axis=1),
+    )
+    qkv_img = jnp.einsum("gpd,dc->gpc", h_pair, w_half, preferred_element_type=jnp.float32)
+    pair_rows = 2 * local_rows
+    half_heads = tile_count // 2
+    qkv_img = qkv_img.reshape(group_count, pair_rows, half_heads, 3, head_dim)
+    log2_scale = score_scale * math.log2(math.e)
+    packed = jnp.stack(
+        [
+            rms_gain(qkv_img[:, :, :, 0, :], q_gain * log2_scale),
+            rms_gain(qkv_img[:, :, :, 1, :], k_gain),
+            qkv_img[:, :, :, 2, :].astype(jnp.bfloat16),
+        ]
+    )
+    packed = jnp.transpose(packed, (3, 2, 0, 1, 4)).reshape(
+        half_heads, pair_rows, 3 * group_count * head_dim
+    )
+    by_head = lax.all_to_all(
+        packed, "tile", split_axis=0, concat_axis=0, tiled=True, axis_index_groups=same_core
+    ).reshape(seq_len, 3 * group_count * head_dim)
     h_txt = modulate(
         text,
         modulation[:, None, 2 * model_width : 3 * model_width],
@@ -98,9 +206,9 @@
     text_queries = jnp.moveaxis(rms_gain(qkv_txt[:, :, :, 0, :], text_q_gain), 2, 1)
     text_keys = jnp.moveaxis(rms_gain(qkv_txt[:, :, :, 1, :], text_k_gain), 2, 1)
     text_values = jnp.moveaxis(qkv_txt[:, :, :, 2, :].astype(jnp.bfloat16), 2, 1)
-    image_queries = jnp.moveaxis(by_head[:, :, :, 0, :], 2, 1)
-    image_keys = jnp.moveaxis(by_head[:, :, :, 1, :], 2, 1)
-    image_values = jnp.moveaxis(by_head[:, :, :, 2, :], 2, 1)
+    by_part = by_head.reshape(seq_len, 3, group_count, head_dim)
+    image_keys = jnp.transpose(by_part[:, 1], (1, 0, 2))[:, None]
+    image_values = jnp.transpose(by_part[:, 2], (1, 0, 2))[:, None]
     slot_live = (jnp.arange(seq_len, dtype=jnp.int32)[None, :] < lengths[:, None]).astype(
         jnp.float32
     )
@@ -124,21 +232,22 @@
         return summed / total[..., None]
 
     text_result = attend_block(text_queries)
-    block_count = seq_len // block
-    query_blocks = jnp.moveaxis(
-        image_queries.reshape(group_count, heads_here, block_count, block, head_dim), 2, 0
-    )
-    image_result = lax.map(attend_block, query_blocks)
-    image_result = jnp.moveaxis(image_result, 0, 2).reshape(
-        group_count, heads_here, seq_len, head_dim
-    )
-    image_result = image_result * slot_live[:, None, :, None]
-    image_heads = (
-        jnp.moveaxis(image_result, 1, 2)
-        .reshape(group_count, seq_len, heads_here * head_dim)
-        .astype(jnp.bfloat16)
-    )
-    image_attention = lax.all_to_all(image_heads, "tile", split_axis=1, concat_axis=2, tiled=True)
+    text_rows = -(-text_len // 128) * 128
+
+    def pack_text(vectors):
+        joined = jnp.moveaxis(vectors[:, 0], 0, 1).reshape(text_len, group_count * head_dim)
+        return jnp.pad(joined, ((0, text_rows - text_len), (0, 0)))
+
+    image_result = attend_image(
+        lengths, by_head, pack_text(text_keys), pack_text(text_values), text_len, group_count, head_dim
+    )
+    sent = image_result.reshape(tile_count, local_rows, group_count * head_dim)
+    got = lax.all_to_all(sent, "tile", split_axis=0, concat_axis=0, tiled=True)
+    image_attention = (
+        got.reshape(tile_count, local_rows, group_count, head_dim)
+        .transpose(2, 1, 0, 3)
+        .reshape(group_count, local_rows, tile_count * head_dim)
+    )
     text_attention = (
         jnp.moveaxis(text_result, 1, 2)
         .reshape(group_count, text_len, heads_here * head_dim)

time: 320 us -> 283 us (0.88)
  matrix products: 86.9 us -> 20.1 us
  Pallas kernels: 0 us -> 43.4 us
  local copies, waits for them, and re-layouts: 43 us -> 28.2 us
  starting transfers between devices: 10.4 us -> 20.6 us
  waiting for transfers between devices: 120 us -> 114 us
    pallas_call x0 -> x1, Pallas kernels: none -> 43.4 us  [attend_image(): pl.pallas_call(functools.partial(attend_kernel, text_len=text_len, groups...]
    dot_general x9 -> x1, matrix products: 39.9 us -> 1.62 us  [attend_block(): jnp.einsum('ghqe,ghke->ghqk', query_block, keys, preferred_element_type=j...]
    dot_general x9 -> x1, matrix products: 30.8 us -> 1.7 us  [attend_block(): jnp.einsum('ghqk,ghke->ghqe', weights.astype(jnp.bfloat16), values, prefe...]
    all_gather x1, waiting for transfers between devices: 72.4 us -> 58 us  [local(): lax.all_gather(turned, ('req', 'tile'), axis=1, tiled=True, axis_index_gr...]
    reshape x3, local copies, waits for them, and re-layouts: 10.5 us -> 2.49 us  [the longest x1 2.28 us: local(): sent = image_result.reshape(tile_count, local_rows, group_count * head_dim)]
    unnamed x33 -> x20, local copies, waits for them, and re-layouts: 10.1 us -> 3.36 us
    ppermute x0 -> x2, waiting for transfers between devices: none -> 5.91 us  [the longest x1 5.9 us: local(): lax.ppermute(w_img, 'tile', [(t, t // 8 * 8 + (t % 8 * 2 + t % 8 // 4) %...]
    all_to_all x2, starting transfers between devices: 10.4 us -> 16.1 us  [the longest x1 11 us: local(): got = lax.all_to_all(sent, 'tile', split_axis=0, concat_axis=0, tiled=True)]
  transfers between devices with their start and end apart: 3 -> 5, of which waited for: 3 -> 4; matrix products, arithmetic and copies ran while one was open for 5% -> 8% of each run, Pallas kernels for 0% -> 0%
where the time goes in v1:
time: 283 us; the launch traced here: 281 us
  waiting for transfers between devices  114 us (40%)
  Pallas kernels  43.4 us (15%)
  local copies, waits for them, and re-layouts  28.2 us (10%)
  blocking collectives  25.1 us (9%)
  starting transfers between devices  20.6 us (7%)
  matrix products  20.1 us (7%)
  other arithmetic  15.7 us (6%)
  between operations  14.4 us (5%)
    all_gather x1, waiting for transfers between devices, local(): lax.all_gather(turned, ('req', 'tile'), axis=1, tiled=True, axis_index_gr...  58 us
    pallas_call x1, Pallas kernels, attend_image(): pl.pallas_call(functools.partial(attend_kernel, text_len=text_len, groups...  43.4 us
    all_to_all x1, waiting for transfers between devices, local(): lax.all_to_all(packed, 'tile', split_axis=0, concat_axis=0, tiled=True, a...  38.3 us
    all_gather x1, blocking collectives, local(): modulation = lax.all_gather(mod_part, 'tile', axis=1, tiled=True)  25.1 us
    dot_general x1, matrix products, local(): jnp.einsum('gpd,dc->gpc', h_pair, w_half, preferred_element_type=jnp.floa...  14.1 us
    all_to_all x1, waiting for transfers between devices, local(): got = lax.all_to_all(sent, 'tile', split_axis=0, concat_axis=0, tiled=True)  11.9 us
    all_to_all x1, starting transfers between devices, local(): got = lax.all_to_all(sent, 'tile', split_axis=0, concat_axis=0, tiled=True)  11 us
    all_to_all x2, local copies, waits for them, and re-layouts, local(): lax.all_to_all(packed, 'tile', split_axis=0, concat_axis=0, tiled=True, a...  10.1 us
  transfers between devices with their start and end apart: 5, of which 4 were waited for; matrix products, arithmetic and copies ran while one was open for 8% of the time, Pallas kernels for 0%

profile of v1, /device:TPU:25, one launch (start us, length us, event | category | flops | bytes accessed | tf_op | source)
XLA Modules:
  0.0 281.4 jit_solution(1238389650229792478)
XLA Ops:
  7.2 4.2 %collective-permute-start.1 = (bf16[2432,48]{0,1:T(8,128)(2,1)}, bf16[2432,48]{0,1:T(8,128)(2,1)S(1)}, u32[]{:S(2)}, u32[]{:S(2)}) collective-permute-start(bf16[2432,48]{0,1:T(8,128)(2,1)} %param.20), channel_id=1, source_target_pairs={{0,0},{1,2},{2,4},{3,6},{4,1},{5,3},{6,5},{7,7},{8,8},{9,10},{10,1... | collective-permute-start | bytes 700424 | tf_op jit(solution)/shard_map/ppermute | solution.py:154
  11.5 5.9 %collective-permute-done.1 = bf16[2432,48]{0,1:T(8,128)(2,1)S(1)} collective-permute-done((bf16[2432,48]{0,1:T(8,128)(2,1)}, bf16[2432,48]{0,1:T(8,128)(2,1)S(1)}, u32[]{:S(2)}, u32[]{:S(2)}) %collective-permute-start.1) | collective-permute-done | bytes 233504 | tf_op jit(solution)/shard_map/ppermute | solution.py:154
  18.9 2.0 fusion.41
  20.8 25.1 %all-gather = bf16[32,304,2]{1,2,0:T(2,128)(2,1)S(1)} all-gather(bf16[1,304,2]{1,2,0:T(2,128)(2,1)S(1)} %fusion.41), channel_id=1, replica_groups=mesh['req'=4,'tile'=32] {'tile'}, dimensions={0}, use_global_device_ids=true | all-gather | bytes 40128 | tf_op jit(solution)/shard_map/all_gather | solution.py:167
  46.1 1.7 convert_reduce_fusion.1
  47.7 1.8 fusion.14
  49.6 3.0 %fusion.17 = bf16[2,128,2432]{2,1,0:T(8,128)(2,1)} fusion(bf16[2,128,2432]{2,1,0:T(8,128)(2,1)} %param.13, f32[2,2432]{1,0:T(2,128)S(1)} %get-tuple-element.17, f32[2,2432]{1,0:T(2,128)S(1)} %get-tuple-element.15, f32[2,128]{1,0:T(2,128)S(1)} %add_rsqrt_fusion.5, f32[2,128]{1,0:T(2,128)S(1)} %broadcast_multiply_fusion.1), kind=kLoop, calls=%fused_computation.24 | loop fusion | flops 3735552 | bytes 2531328 | tf_op jit(solution)/shard_map/convert_element_type | solution.py:26
  54.0 2.1 fusion.6
  56.1 3.0 %fusion.9 = bf16[2,154,2432]{2,0,1:T(2,128)(2,1)S(1)} fusion(bf16[2,154,2432]{2,0,1:T(2,128)(2,1)S(1)} %copy-done.1, f32[2,2432]{1,0:T(2,128)S(1)} %get-tuple-element.16, f32[2,2432]{1,0:T(2,128)S(1)} %get-tuple-element.14, f32[2,154]{0,1:T(8,128)S(1)} %add_rsqrt_fusion, f32[2,154]{0,1:T(8,128)S(1)} %broadcast_multiply_fusion), kind=kLoop, calls=%fused_computation.16 | loop fusion | flops 4494336 | bytes 3037600 | tf_op jit(solution)/shard_map/convert_element_type | solution.py:26
  59.8 58.0 %all-gather.3.cloned.1.call-done = bf16[2432,3072]{0,1:T(8,128)(2,1)} async-done(((bf16[2432,48]{0,1:T(8,128)(2,1)}), bf16[2432,3072]{0,1:T(8,128)(2,1)}) %all-gather.3.cloned.1.call-update) | async-done | bytes 14942224 | tf_op jit(solution)/shard_map/all_gather | solution.py:159
  117.8 14.1 %fusion = f32[2,256,3072]{1,2,0:T(8,128)S(1)} fusion(bf16[2432,3072]{0,1:T(8,128)(2,1)} %all-gather.3.cloned.1.call-done, bf16[2,128,2432]{2,1,0:T(8,128)(2,1)} %collective-permute-done, bf16[2,128,2432]{2,1,0:T(8,128)(2,1)} %fusion.17, pred[]{:T(512)S(6)} %eq.5), kind=kOutput, calls=%fused_computation | convolution fusion | flops 7661617152 | bytes 23724032 | tf_op jit(solution)/shard_map/gpd,dc->gpc/dot_general | solution.py:180
  134.1 2.1 copy.89
  136.2 5.2 %all-to-all-start = ((bf16[16,256,384]{1,2,0:T(8,128)(2,1)}), bf16[16,256,384]{1,2,0:T(8,128)(2,1)}, u32[]{:S(2)}, u32[]{:S(2)}) async-start(bf16[16,256,384]{1,2,0:T(8,128)(2,1)} %bitcast.118), calls=%async_computation | async-start | bytes 6291456 | tf_op jit(solution)/shard_map/all_to_all | solution.py:195
  143.4 38.3 %all-to-all-done = bf16[16,256,384]{1,2,0:T(8,128)(2,1)} async-done(((bf16[16,256,384]{1,2,0:T(8,128)(2,1)}), bf16[16,256,384]{1,2,0:T(8,128)(2,1)}, u32[]{:S(2)}, u32[]{:S(2)}) %all-to-all-start) | async-done | bytes 3145760 | tf_op jit(solution)/shard_map/all_to_all | solution.py:195
  181.7 5.4 %copy.103 = bf16[16,256,384]{1,0,2:T(8,128)(2,1)} copy(bf16[16,256,384]{1,2,0:T(8,128)(2,1)} %all-to-all-done) | data formatting | bytes 6291456 | tf_op jit(solution)/shard_map/all_to_all | solution.py:195
  187.1 5.9 %reshape_reshape.3 = bf16[4096,3,2,64]{0,3,2,1:T(8,128)(2,1)} reshape(bf16[16,256,384]{1,0,2:T(8,128)(2,1)} %copy.103) | data formatting | bytes 6291456 | tf_op jit(solution)/shard_map/reshape;reshape | solution.py:209
  192.9 4.7 %copy.90 = bf16[16,256,384]{2,1,0:T(8,128)(2,1)} copy(bf16[16,256,384]{1,2,0:T(8,128)(2,1)} %all-to-all-done) | data formatting | bytes 6291456 | tf_op jit(solution)/shard_map/all_to_all | solution.py:195
  197.7 43.4 %shard_map.140 = bf16[4096,128]{1,0:T(8,128)(2,1)} custom-call(s32[2]{0:T(128)} %lengths_ref.1, bf16[4096,384]{1,0:T(8,128)(2,1)} %bitcast.111, bf16[4096,384]{1,0:T(8,128)(2,1)} %bitcast.112, bf16[4096,384]{1,0:T(8,128)(2,1)} %bitcast.113, bf16[256,128]{1,0:T(8,128)(2,1)} %pad.9.text_key_ref, bf16[256,128]{1,0:T(8,128)(2,1)} %pad.10.text_value_ref), custom_call_target="tpu_custom_call" | custom-call | tf_op jit(solution)/shard_map/pallas_call | solution.py:105
  241.0 2.3 copy.101
  243.3 11.0 %all-to-all-start.1 = ((bf16[32,128,128]{1,2,0:T(8,128)(2,1)}), bf16[32,128,128]{1,2,0:T(8,128)(2,1)S(1)}, u32[]{:S(2)}, u32[]{:S(2)}) async-start(bf16[32,128,128]{1,2,0:T(8,128)(2,1)} %copy.101), calls=%async_computation.1 | async-start | bytes 2097152 | tf_op jit(solution)/shard_map/all_to_all | solution.py:245
  254.3 1.7 slice_bitcast_fusion
  257.6 1.7 fusion.34
  259.3 11.9 %all-to-all-done.1 = bf16[32,128,128]{1,2,0:T(8,128)(2,1)S(1)} async-done(((bf16[32,128,128]{1,2,0:T(8,128)(2,1)}), bf16[32,128,128]{1,2,0:T(8,128)(2,1)S(1)}, u32[]{:S(2)}, u32[]{:S(2)}) %all-to-all-start.1) | async-done | bytes 1048608 | tf_op jit(solution)/shard_map/all_to_all | solution.py:245
  272.3 2.3 copy.104
  (58 shorter events, 10.6 us)
Async XLA Ops:
  7.2 11.7 %copy-start = (bf16[2432,304]{0,1:T(8,128)(2,1)S(1)}, bf16[2432,304]{0,1:T(8,128)(2,1)}, u32[]{:S(2)}) copy-start(bf16[2432,304]{0,1:T(8,128)(2,1)} %param.19) | copy-start | bytes 4435972
  7.2 110.6 %all-gather.3.cloned.1.call-start = ((), (), s32[]{:S(2)}) async-start(), calls=%async_computation.2 | async-start | bytes 15175680 | tf_op jit(solution)/shard_map/all_gather | solution.py:159
  7.2 10.1 %collective-permute-start.1 = (bf16[2432,48]{0,1:T(8,128)(2,1)}, bf16[2432,48]{0,1:T(8,128)(2,1)S(1)}, u32[]{:S(2)}, u32[]{:S(2)}) collective-permute-start(bf16[2432,48]{0,1:T(8,128)(2,1)} %param.20), channel_id=1, source_target_pairs={{0,0},{1,2},{2,4},{3,6},{4,1},{5,3},{6,5},{7,7},{8,8},{9,10},{10,1... | collective-permute-start | bytes 700424 | tf_op jit(solution)/shard_map/ppermute | solution.py:154
  17.4 0.7 copy-start.2
  46.1 6.6 %copy-start.1 = (bf16[2,154,2432]{2,0,1:T(2,128)(2,1)S(1)}, bf16[2,154,2432]{2,0,1:T(2,128)(2,1)}, u32[]{:S(2)}) copy-start(bf16[2,154,2432]{2,0,1:T(2,128)(2,1)} %param.14) | copy-start | bytes 4494340
  49.6 6.5 %copy-start.7 = (f32[64]{0:T(128)S(1)}, f32[64]{0:T(128)}, u32[]{:S(2)}) copy-start(f32[64]{0:T(128)} %param.22) | copy-start | bytes 772
  52.5 7.3 %collective-permute-start = (bf16[2,128,2432]{2,1,0:T(8,128)(2,1)}, bf16[2,128,2432]{2,1,0:T(8,128)(2,1)}, u32[]{:S(2)}, u32[]{:S(2)}) collective-permute-start(bf16[2,128,2432]{2,1,0:T(8,128)(2,1)} %fusion.17), channel_id=1, source_target_pairs={{0,1},{1,0},{2,3},{3,2},{4,5},{5,4},{6,7},{7,6},{8,9},{9,8},{10,11... | collective-permute-start | bytes 3735560 | tf_op jit(solution)/shard_map/ppermute | solution.py:174
  53.9 5.1 %copy-start.6 = (bf16[2432,192]{0,1:T(8,128)(2,1)S(1)}, bf16[2432,192]{0,1:T(8,128)(2,1)}, u32[]{:S(2)}) copy-start(bf16[2432,192]{0,1:T(8,128)(2,1)} %param.21) | copy-start | bytes 2801668
  132.2 0.7 copy-start.5
  136.2 5.2 %copy-start.3 = (f32[64]{0:T(128)S(1)}, f32[64]{0:T(128)}, u32[]{:S(2)}) copy-start(f32[64]{0:T(128)} %param.25) | copy-start | bytes 772
  136.2 7.0 %copy-start.4 = (s32[2]{0:T(128)S(1)}, s32[2]{0:T(128)}, u32[]{:S(2)}) copy-start(s32[2]{0:T(128)} %lengths_ref.1) | copy-start | bytes 28
  136.2 45.5 %all-to-all-start = ((bf16[16,256,384]{1,2,0:T(8,128)(2,1)}), bf16[16,256,384]{1,2,0:T(8,128)(2,1)}, u32[]{:S(2)}, u32[]{:S(2)}) async-start(bf16[16,256,384]{1,2,0:T(8,128)(2,1)} %bitcast.118), calls=%async_computation | async-start | bytes 6291456 | tf_op jit(solution)/shard_map/all_to_all | solution.py:195
  243.3 27.9 %all-to-all-start.1 = ((bf16[32,128,128]{1,2,0:T(8,128)(2,1)}), bf16[32,128,128]{1,2,0:T(8,128)(2,1)S(1)}, u32[]{:S(2)}, u32[]{:S(2)}) async-start(bf16[32,128,128]{1,2,0:T(8,128)(2,1)} %copy.101), calls=%async_computation.1 | async-start | bytes 2097152 | tf_op jit(solution)/shard_map/all_to_all | solution.py:245
  254.3 1.7 copy-start.8
Sparse Core Ops, SparseCore 0:
  18.2 99.5 all-gather.2

commit v2 on v1

--- a/solution.py
+++ b/solution.py
@@ -35,10 +35,10 @@
 
 LANES = 128
 QUERY_BLOCK = 512
-KEY_BLOCK = 512
-
-
-def attend_kernel(lengths_ref, query_ref, key_ref, value_ref, text_key_ref, text_value_ref, out_ref, aug_ref, text_aug_ref, *, text_len, groups, width):
+KEY_BLOCK = 1024
+
+
+def attend_kernel(lengths_ref, query_ref, key_ref, value_ref, text_query_ref, text_key_ref, text_value_ref, out_ref, text_out_ref, aug_ref, text_aug_ref, *, text_len, groups, width):
     step = pl.program_id(0)
     rows = query_ref.shape[0]
     seq_len = key_ref.shape[0]
@@ -66,40 +66,50 @@
 
             lax.fori_loop(0, seq_len // KEY_BLOCK, fill, 0)
 
-    lane = lax.broadcasted_iota(jnp.int32, (rows, LANES), 1) // width
+    def attend(query_from, group):
+        lane = lax.broadcasted_iota(jnp.int32, query_from.shape, 1) // width
+        query = jnp.where(lane == group, query_from[...].astype(jnp.float32), 0.0).astype(
+            jnp.bfloat16
+        )
+
+        def part(keys, augmented):
+            scores = lax.dot_general(
+                query, keys, (((1,), (1,)), ((), ())), preferred_element_type=jnp.float32
+            )
+            weights = jnp.exp2(scores).astype(jnp.bfloat16)
+            return jnp.dot(weights, augmented, preferred_element_type=jnp.float32)
+
+        def body(index, acc):
+            start = pl.multiple_of(index * KEY_BLOCK, KEY_BLOCK)
+            return acc + part(
+                key_ref[pl.ds(start, KEY_BLOCK), :], aug_ref[group, pl.ds(start, KEY_BLOCK), :]
+            )
+
+        acc = part(text_key_ref[...], text_aug_ref[group])
+        acc = lax.fori_loop(0, (lengths_ref[group] + KEY_BLOCK - 1) // KEY_BLOCK, body, acc)
+        return acc / pltpu.roll(acc, LANES // 2, 1), lane == group
+
+    @pl.when(step == 0)
+    def _():
+        joined = jnp.zeros(text_out_ref.shape, jnp.float32)
+        for group in range(groups):
+            result, own = attend(text_query_ref, group)
+            joined = jnp.where(own, result, joined)
+        text_out_ref[...] = joined.astype(jnp.bfloat16)
+
+    out_ref[...] = jnp.zeros_like(out_ref)
     row = lax.broadcasted_iota(jnp.int32, (rows, LANES), 0) + step * rows
-    out_ref[...] = jnp.zeros_like(out_ref)
     for group in range(groups):
         length = lengths_ref[group]
 
         @pl.when(step * rows < length)
         def _():
-            query = jnp.where(lane == group, query_ref[...].astype(jnp.float32), 0.0).astype(
-                jnp.bfloat16
-            )
-
-            def part(keys, augmented):
-                scores = lax.dot_general(
-                    query, keys, (((1,), (1,)), ((), ())), preferred_element_type=jnp.float32
-                )
-                weights = jnp.exp2(scores).astype(jnp.bfloat16)
-                return jnp.dot(weights, augmented, preferred_element_type=jnp.float32)
-
-            def body(index, acc):
-                start = pl.multiple_of(index * KEY_BLOCK, KEY_BLOCK)
-                return acc + part(
-                    key_ref[pl.ds(start, KEY_BLOCK), :],
-                    aug_ref[group, pl.ds(start, KEY_BLOCK), :],
-                )
-
-            acc = part(text_key_ref[...], text_aug_ref[group])
-            acc = lax.fori_loop(0, (length + KEY_BLOCK - 1) // KEY_BLOCK, body, acc)
-            total = pltpu.roll(acc, LANES // 2, 1)
-            result = jnp.where(row < length, acc / total, 0.0).astype(jnp.bfloat16)
-            out_ref[...] = jnp.where(lane == group, result, out_ref[...])
-
-
-def attend_image(lengths, by_head, text_key, text_value, text_len, groups, width):
+            result, own = attend(query_ref, group)
+            result = jnp.where(row < length, result, 0.0).astype(jnp.bfloat16)
+            out_ref[...] = jnp.where(own, result, out_ref[...])
+
+
+def attend_image(lengths, by_head, text_query, text_key, text_value, text_len, groups, width):
     seq_len = by_head.shape[0]
     text_rows = text_key.shape[0]
     return pl.pallas_call(
@@ -113,15 +123,22 @@
                 pl.BlockSpec((seq_len, LANES), lambda i, n: (0, 2)),
                 pl.BlockSpec((text_rows, LANES), lambda i, n: (0, 0)),
                 pl.BlockSpec((text_rows, LANES), lambda i, n: (0, 0)),
+                pl.BlockSpec((text_rows, LANES), lambda i, n: (0, 0)),
             ],
-            out_specs=pl.BlockSpec((QUERY_BLOCK, LANES), lambda i, n: (i, 0)),
+            out_specs=[
+                pl.BlockSpec((QUERY_BLOCK, LANES), lambda i, n: (i, 0)),
+                pl.BlockSpec((text_rows, LANES), lambda i, n: (0, 0)),
+            ],
             scratch_shapes=[
                 pltpu.VMEM((groups, seq_len, LANES), jnp.bfloat16),
                 pltpu.VMEM((groups, text_rows, LANES), jnp.bfloat16),
             ],
         ),
-        out_shape=jax.ShapeDtypeStruct((seq_len, LANES), jnp.bfloat16),
-    )(lengths, by_head, by_head, by_head, text_key, text_value)
+        out_shape=[
+            jax.ShapeDtypeStruct((seq_len, LANES), jnp.bfloat16),
+            jax.ShapeDtypeStruct((text_rows, LANES), jnp.bfloat16),
+        ],
+    )(lengths, by_head, by_head, by_head, text_query, text_key, text_value)
 
 
 def local(
@@ -203,43 +220,24 @@
     qkv_txt = jnp.einsum("gtd,dc->gtc", h_txt, w_txt, preferred_element_type=jnp.float32).reshape(
         group_count, text_len, heads_here, 3, head_dim
     )
-    text_queries = jnp.moveaxis(rms_gain(qkv_txt[:, :, :, 0, :], text_q_gain), 2, 1)
+    text_queries = jnp.moveaxis(rms_gain(qkv_txt[:, :, :, 0, :], text_q_gain * log2_scale), 2, 1)
     text_keys = jnp.moveaxis(rms_gain(qkv_txt[:, :, :, 1, :], text_k_gain), 2, 1)
     text_values = jnp.moveaxis(qkv_txt[:, :, :, 2, :].astype(jnp.bfloat16), 2, 1)
-    by_part = by_head.reshape(seq_len, 3, group_count, head_dim)
-    image_keys = jnp.transpose(by_part[:, 1], (1, 0, 2))[:, None]
-    image_values = jnp.transpose(by_part[:, 2], (1, 0, 2))[:, None]
-    slot_live = (jnp.arange(seq_len, dtype=jnp.int32)[None, :] < lengths[:, None]).astype(
-        jnp.float32
-    )
-    keys = jnp.concatenate([text_keys, image_keys], axis=2)
-    values = jnp.concatenate([text_values, image_values], axis=2)
-    key_mask = jnp.concatenate([jnp.ones((group_count, text_len), jnp.float32), slot_live], axis=1)
-
-    def attend_block(query_block):
-        scores = (
-            jnp.einsum("ghqe,ghke->ghqk", query_block, keys, preferred_element_type=jnp.float32)
-            * score_scale
-        )
-        weights = jnp.exp(scores) * key_mask[:, None, None, :]
-        total = jnp.sum(weights, axis=-1)
-        summed = jnp.einsum(
-            "ghqk,ghke->ghqe",
-            weights.astype(jnp.bfloat16),
-            values,
-            preferred_element_type=jnp.float32,
-        )
-        return summed / total[..., None]
-
-    text_result = attend_block(text_queries)
     text_rows = -(-text_len // 128) * 128
 
     def pack_text(vectors):
         joined = jnp.moveaxis(vectors[:, 0], 0, 1).reshape(text_len, group_count * head_dim)
         return jnp.pad(joined, ((0, text_rows - text_len), (0, 0)))
 
-    image_result = attend_image(
-        lengths, by_head, pack_text(text_keys), pack_text(text_values), text_len, group_count, head_dim
+    image_result, text_result = attend_image(
+        lengths,
+        by_head,
+        pack_text(text_queries),
+        pack_text(text_keys),
+        pack_text(text_values),
+        text_len,
+        group_count,
+        head_dim,
     )
     sent = image_result.reshape(tile_count, local_rows, group_count * head_dim)
     got = lax.all_to_all(sent, "tile", split_axis=0, concat_axis=0, tiled=True)
@@ -248,10 +246,8 @@
         .transpose(2, 1, 0, 3)
         .reshape(group_count, local_rows, tile_count * head_dim)
     )
-    text_attention = (
-        jnp.moveaxis(text_result, 1, 2)
-        .reshape(group_count, text_len, heads_here * head_dim)
-        .astype(jnp.bfloat16)
+    text_attention = jnp.moveaxis(
+        text_result[:text_len].reshape(text_len, group_count, head_dim), 1, 0
     )
     return (image_attention, text_attention)
 

time: 283 us -> 270 us (0.954)
  local copies, waits for them, and re-layouts: 28.2 us -> 16.8 us
  waiting for transfers between devices: 114 us -> 122 us
  other arithmetic: 15.7 us -> 11.4 us
  matrix products: 20.1 us -> 16.1 us
    all_gather x1, waiting for transfers between devices: 58 us -> 66.1 us  [local(): lax.all_gather(turned, ('req', 'tile'), axis=1, tiled=True, axis_index_gr...]
    all_to_all x1, waiting for transfers between devices: 38.3 us -> 30.8 us  [local(): lax.all_to_all(packed, 'tile', split_axis=0, concat_axis=0, tiled=True, a...]
    another operation x1 -> x0, local copies, waits for them, and re-layouts: 5.87 us -> none  [local(): by_part = by_head.reshape(seq_len, 3, group_count, head_dim)]
    all_to_all x2 -> x1, local copies, waits for them, and re-layouts: 10.1 us -> 4.65 us  [local(): lax.all_to_all(packed, 'tile', split_axis=0, concat_axis=0, tiled=True, a...]
    all_to_all x1, waiting for transfers between devices: 11.9 us -> 16 us  [local(): got = lax.all_to_all(sent, 'tile', split_axis=0, concat_axis=0, tiled=True)]
    dot_general x2 -> x0, matrix products: 3.32 us -> none  [the longest x1 1.7 us: attend_block(): jnp.einsum('ghqk,ghke->ghqe', weights.astype(jnp.bfloat16), values, prefe...]
    ppermute x1, waiting for transfers between devices: 0.01 us -> 2.98 us  [local(): lax.ppermute(h_img, 'tile', [(t, t ^ 1) for t in range(tile_count)])]
  transfers between devices with their start and end apart: 5 -> 5, of which waited for: 4 -> 5; matrix products, arithmetic and copies ran while one was open for 8% -> 6% of each run, Pallas kernels for 0% -> 0%
where the time goes in v2:
time: 270 us
  waiting for transfers between devices  122 us (45%)
  Pallas kernels  43.8 us (16%)
  blocking collectives  25.1 us (9%)
  starting transfers between devices  20.6 us (8%)
  local copies, waits for them, and re-layouts  16.8 us (6%)
  matrix products  16.1 us (6%)
  between operations  14.4 us (5%)
  other arithmetic  11.4 us (4%)
    all_gather x1, waiting for transfers between devices, local(): lax.all_gather(turned, ('req', 'tile'), axis=1, tiled=True, axis_index_gr...  66.1 us
    pallas_call x1, Pallas kernels, attend_image(): pl.pallas_call(functools.partial(attend_kernel, text_len=text_len, groups...  43.8 us
    all_to_all x1, waiting for transfers between devices, local(): lax.all_to_all(packed, 'tile', split_axis=0, concat_axis=0, tiled=True, a...  30.8 us
    all_gather x1, blocking collectives, local(): modulation = lax.all_gather(mod_part, 'tile', axis=1, tiled=True)  25.1 us
    all_to_all x1, waiting for transfers between devices, local(): got = lax.all_to_all(sent, 'tile', split_axis=0, concat_axis=0, tiled=True)  16 us
    dot_general x1, matrix products, local(): jnp.einsum('gpd,dc->gpc', h_pair, w_half, preferred_element_type=jnp.floa...  13.4 us
    all_to_all x1, starting transfers between devices, local(): got = lax.all_to_all(sent, 'tile', split_axis=0, concat_axis=0, tiled=True)  11 us
    ppermute x1, waiting for transfers between devices, local(): lax.ppermute(w_img, 'tile', [(t, t // 8 * 8 + (t % 8 * 2 + t % 8 // 4) %...  5.9 us
  transfers between devices with their start and end apart: 5, of which 5 were waited for; matrix products, arithmetic and copies ran while one was open for 6% of the time, Pallas kernels for 0%

profile of v2, /device:TPU:25, one launch (start us, length us, event | category | flops | bytes accessed | tf_op | source)
XLA Modules:
  0.0 269.8 jit_solution(4042453773732710882)
XLA Ops:
  7.2 4.2 %collective-permute-start.1 = (bf16[2432,48]{0,1:T(8,128)(2,1)}, bf16[2432,48]{0,1:T(8,128)(2,1)S(1)}, u32[]{:S(2)}, u32[]{:S(2)}) collective-permute-start(bf16[2432,48]{0,1:T(8,128)(2,1)} %param.20), channel_id=1, source_target_pairs={{0,0},{1,2},{2,4},{3,6},{4,1},{5,3},{6,5},{7,7},{8,8},{9,10},{10,1... | collective-permute-start | bytes 700424 | tf_op jit(solution)/shard_map/ppermute | solution.py:171
  11.5 5.9 %collective-permute-done.1 = bf16[2432,48]{0,1:T(8,128)(2,1)S(1)} collective-permute-done((bf16[2432,48]{0,1:T(8,128)(2,1)}, bf16[2432,48]{0,1:T(8,128)(2,1)S(1)}, u32[]{:S(2)}, u32[]{:S(2)}) %collective-permute-start.1) | collective-permute-done | bytes 233504 | tf_op jit(solution)/shard_map/ppermute | solution.py:171
  17.4 0.7 copy-done.3
  18.9 2.0 fusion.27
  20.8 25.1 %all-gather = bf16[32,304,2]{1,2,0:T(2,128)(2,1)S(1)} all-gather(bf16[1,304,2]{1,2,0:T(2,128)(2,1)S(1)} %fusion.27), channel_id=1, replica_groups=mesh['req'=4,'tile'=32] {'tile'}, dimensions={0}, use_global_device_ids=true | all-gather | bytes 40128 | tf_op jit(solution)/shard_map/all_gather | solution.py:184
  46.9 1.7 fusion.13
  48.7 3.0 %collective-permute-done = bf16[2,128,2432]{2,1,0:T(8,128)(2,1)S(1)} collective-permute-done((bf16[2,128,2432]{2,1,0:T(8,128)(2,1)}, bf16[2,128,2432]{2,1,0:T(8,128)(2,1)S(1)}, u32[]{:S(2)}, u32[]{:S(2)}) %collective-permute-start) | collective-permute-done | bytes 1245216 | tf_op jit(solution)/shard_map/ppermute | solution.py:191
  51.7 66.1 %all-gather.3.cloned.1.call-done = bf16[2432,3072]{0,1:T(8,128)(2,1)} async-done(((bf16[2432,48]{0,1:T(8,128)(2,1)}), bf16[2432,3072]{0,1:T(8,128)(2,1)}) %all-gather.3.cloned.1.call-update) | async-done | bytes 14942224 | tf_op jit(solution)/shard_map/all_gather | solution.py:176
  117.8 13.4 %fusion = f32[2,256,3072]{1,2,0:T(8,128)S(1)} fusion(bf16[2432,3072]{0,1:T(8,128)(2,1)} %all-gather.3.cloned.1.call-done, bf16[2,128,2432]{2,1,0:T(8,128)(2,1)S(1)} %collective-permute-done, bf16[2,128,2432]{2,1,0:T(8,128)(2,1)} %fusion.13, pred[]{:T(512)S(6)} %eq.5), kind=kOutput, calls=%fused_computation | convolution fusion | flops 7661617152 | bytes 23724032 | tf_op jit(solution)/shard_map/gpd,dc->gpc/dot_general | solution.py:197
  132.1 0.9 fusion.21
  133.4 2.1 copy.78
  135.5 5.2 %all-to-all-start = ((bf16[16,256,384]{1,2,0:T(8,128)(2,1)}), bf16[16,256,384]{1,2,0:T(8,128)(2,1)}, u32[]{:S(2)}, u32[]{:S(2)}) async-start(bf16[16,256,384]{1,2,0:T(8,128)(2,1)} %bitcast.76), calls=%async_computation | async-start | bytes 6291456 | tf_op jit(solution)/shard_map/all_to_all | solution.py:212
  140.7 1.2 convert_reduce_fusion
  141.9 2.1 fusion.4
  144.1 3.0 %fusion.7 = bf16[2,154,2432]{2,0,1:T(2,128)(2,1)S(1)} fusion(bf16[2,154,2432]{2,0,1:T(2,128)(2,1)S(1)} %copy-done.1, f32[2,2432]{1,0:T(2,128)S(1)} %get-tuple-element.22, f32[2,2432]{1,0:T(2,128)S(1)} %get-tuple-element.20, f32[2,154]{0,1:T(8,128)S(1)} %add_rsqrt_fusion, f32[2,154]{0,1:T(8,128)S(1)} %broadcast_multiply_fusion), kind=kLoop, calls=%fused_computation.13 | loop fusion | flops 4494336 | bytes 3037600 | tf_op jit(solution)/shard_map/convert_element_type | solution.py:26
  150.2 30.8 %all-to-all-done = bf16[16,256,384]{1,2,0:T(8,128)(2,1)} async-done(((bf16[16,256,384]{1,2,0:T(8,128)(2,1)}), bf16[16,256,384]{1,2,0:T(8,128)(2,1)}, u32[]{:S(2)}, u32[]{:S(2)}) %all-to-all-start) | async-done | bytes 3145760 | tf_op jit(solution)/shard_map/all_to_all | solution.py:212
  181.0 4.7 %copy.79 = bf16[16,256,384]{2,1,0:T(8,128)(2,1)} copy(bf16[16,256,384]{1,2,0:T(8,128)(2,1)} %all-to-all-done) | data formatting | bytes 6291456 | tf_op jit(solution)/shard_map/all_to_all | solution.py:212
  185.7 43.8 %shard_map.140 = (bf16[4096,128]{1,0:T(8,128)(2,1)}, bf16[256,128]{1,0:T(8,128)(2,1)}) custom-call(s32[2]{0:T(128)} %lengths_ref.1, bf16[4096,384]{1,0:T(8,128)(2,1)} %bitcast.69, bf16[4096,384]{1,0:T(8,128)(2,1)} %bitcast.70, bf16[4096,384]{1,0:T(8,128)(2,1)} %bitcast.71, bf16[256,128]{1,0:T(8,128)(2,1)} %pad.10.text_query_ref, ...), custom_call_target="tpu_custom_call" | custom-call | tf_op jit(solution)/shard_map/pallas_call | solution.py:115
  229.4 2.3 copy.89
  231.7 11.0 %all-to-all-start.1 = ((bf16[32,128,128]{1,2,0:T(8,128)(2,1)}), bf16[32,128,128]{1,2,0:T(8,128)(2,1)S(1)}, u32[]{:S(2)}, u32[]{:S(2)}) async-start(bf16[32,128,128]{1,2,0:T(8,128)(2,1)} %copy.89), calls=%async_computation.1 | async-start | bytes 2097152 | tf_op jit(solution)/shard_map/all_to_all | solution.py:243
  242.9 0.7 copy.92
  243.7 16.0 %all-to-all-done.1 = bf16[32,128,128]{1,2,0:T(8,128)(2,1)S(1)} async-done(((bf16[32,128,128]{1,2,0:T(8,128)(2,1)}), bf16[32,128,128]{1,2,0:T(8,128)(2,1)S(1)}, u32[]{:S(2)}, u32[]{:S(2)}) %all-to-all-start.1) | async-done | bytes 1048608 | tf_op jit(solution)/shard_map/all_to_all | solution.py:243
  259.7 1.0 copy.90
  260.7 2.3 copy.91
  (55 shorter events, 6.4 us)
Async XLA Ops:
  7.2 11.7 %copy-start = (bf16[2432,304]{0,1:T(8,128)(2,1)S(1)}, bf16[2432,304]{0,1:T(8,128)(2,1)}, u32[]{:S(2)}) copy-start(bf16[2432,304]{0,1:T(8,128)(2,1)} %param.19) | copy-start | bytes 4435972
  7.2 38.9 %copy-start.2 = (bf16[2,128,2432]{2,1,0:T(8,128)(2,1)S(1)}, bf16[2,128,2432]{2,1,0:T(8,128)(2,1)}, u32[]{:S(2)}) copy-start(bf16[2,128,2432]{2,1,0:T(8,128)(2,1)} %param.13) | copy-start | bytes 3735556
  7.2 110.6 %all-gather.3.cloned.1.call-start = ((), (), s32[]{:S(2)}) async-start(), calls=%async_computation.2 | async-start | bytes 15175680 | tf_op jit(solution)/shard_map/all_gather | solution.py:176
  7.2 10.1 %collective-permute-start.1 = (bf16[2432,48]{0,1:T(8,128)(2,1)}, bf16[2432,48]{0,1:T(8,128)(2,1)S(1)}, u32[]{:S(2)}, u32[]{:S(2)}) collective-permute-start(bf16[2432,48]{0,1:T(8,128)(2,1)} %param.20), channel_id=1, source_target_pairs={{0,0},{1,2},{2,4},{3,6},{4,1},{5,3},{6,5},{7,7},{8,8},{9,10},{10,1... | collective-permute-start | bytes 700424 | tf_op jit(solution)/shard_map/ppermute | solution.py:171
  17.4 0.7 copy-start.3
  46.1 2.7 copy-start.8
  48.6 3.2 %collective-permute-start = (bf16[2,128,2432]{2,1,0:T(8,128)(2,1)}, bf16[2,128,2432]{2,1,0:T(8,128)(2,1)S(1)}, u32[]{:S(2)}, u32[]{:S(2)}) collective-permute-start(bf16[2,128,2432]{2,1,0:T(8,128)(2,1)} %fusion.13), channel_id=1, source_target_pairs={{0,1},{1,0},{2,3},{3,2},{4,5},{5,4},{6,7},{7,6},{8,9},{9,8},{10,11... | collective-permute-start | bytes 3735560 | tf_op jit(solution)/shard_map/ppermute | solution.py:191
  131.5 0.7 copy-start.6
  135.5 5.2 %copy-start.1 = (bf16[2,154,2432]{2,0,1:T(2,128)(2,1)S(1)}, bf16[2,154,2432]{2,0,1:T(2,128)(2,1)}, u32[]{:S(2)}) copy-start(bf16[2,154,2432]{2,0,1:T(2,128)(2,1)} %param.14) | copy-start | bytes 4494340
  135.5 45.5 %all-to-all-start = ((bf16[16,256,384]{1,2,0:T(8,128)(2,1)}), bf16[16,256,384]{1,2,0:T(8,128)(2,1)}, u32[]{:S(2)}, u32[]{:S(2)}) async-start(bf16[16,256,384]{1,2,0:T(8,128)(2,1)} %bitcast.76), calls=%async_computation | async-start | bytes 6291456 | tf_op jit(solution)/shard_map/all_to_all | solution.py:212
  141.9 5.1 %copy-start.7 = (bf16[2432,192]{0,1:T(8,128)(2,1)S(1)}, bf16[2432,192]{0,1:T(8,128)(2,1)}, u32[]{:S(2)}) copy-start(bf16[2432,192]{0,1:T(8,128)(2,1)} %param.21) | copy-start | bytes 2801668
  147.0 0.8 copy-start.9
  147.0 0.8 copy-start.5
  229.4 13.3 %copy-start.4 = (bf16[256,128]{1,0:T(8,128)(2,1)S(1)}, bf16[256,128]{1,0:T(8,128)(2,1)}, u32[]{:S(2)}) copy-start(bf16[256,128]{1,0:T(8,128)(2,1)} %get-tuple-element.5) | copy-start | bytes 196612
  231.7 27.9 %all-to-all-start.1 = ((bf16[32,128,128]{1,2,0:T(8,128)(2,1)}), bf16[32,128,128]{1,2,0:T(8,128)(2,1)S(1)}, u32[]{:S(2)}, u32[]{:S(2)}) async-start(bf16[32,128,128]{1,2,0:T(8,128)(2,1)} %copy.89), calls=%async_computation.1 | async-start | bytes 2097152 | tf_op jit(solution)/shard_map/all_to_all | solution.py:243
Sparse Core Ops, SparseCore 0:
  18.2 99.5 all-gather.2

commit v3 on v2

--- a/solution.py
+++ b/solution.py
@@ -163,18 +163,26 @@
     head_dim = q_gain.shape[0]
     heads_here = w_txt.shape[1] // (3 * head_dim)
     score_scale = head_dim ** (-0.5)
-    same_core = [[t for t in range(tile_count) if t % 2 == c] for c in range(2)]
-    all_same_core = [
-        [r * tile_count + t for r in range(lax.axis_size("req")) for t in same_core[c]]
-        for c in range(2)
+    req_count = lax.axis_size("req")
+    plane = tile_count // req_count
+    lines = [[x * plane + p for x in range(req_count)] for p in range(plane)]
+    planes = [[x * plane + p for p in range(plane)] for x in range(req_count)]
+    all_planes = [
+        [r * tile_count + t for r in range(req_count) for t in planes[x]] for x in range(req_count)
     ]
+    image = lax.all_gather(image, "tile", axis=1, tiled=True, axis_index_groups=lines)
     turned = lax.ppermute(
         w_img,
-        "tile",
-        [(t, t // 8 * 8 + ((t % 8) * 2 + (t % 8) // 4) % 8) for t in range(tile_count)],
-    )
-    w_half = lax.all_gather(
-        turned, ("req", "tile"), axis=1, tiled=True, axis_index_groups=all_same_core
+        ("req", "tile"),
+        [
+            (r * tile_count + x * plane + p, x * tile_count + r * plane + p)
+            for r in range(req_count)
+            for x in range(req_count)
+            for p in range(plane)
+        ],
+    )
+    w_part = lax.all_gather(
+        turned, ("req", "tile"), axis=1, tiled=True, axis_index_groups=all_planes
     )
     features = time_features(timesteps, w_time.shape[0])
     cond_act = jax.nn.silu(
@@ -187,17 +195,9 @@
         modulation[:, None, 0:model_width],
         modulation[:, None, model_width : 2 * model_width],
     )
-    core = lax.axis_index("tile") % 2
-    h_other = lax.ppermute(h_img, "tile", [(t, t ^ 1) for t in range(tile_count)])
-    h_pair = jnp.where(
-        core == 0,
-        jnp.concatenate([h_img, h_other], axis=1),
-        jnp.concatenate([h_other, h_img], axis=1),
-    )
-    qkv_img = jnp.einsum("gpd,dc->gpc", h_pair, w_half, preferred_element_type=jnp.float32)
-    pair_rows = 2 * local_rows
-    half_heads = tile_count // 2
-    qkv_img = qkv_img.reshape(group_count, pair_rows, half_heads, 3, head_dim)
+    qkv_img = jnp.einsum("gpd,dc->gpc", h_img, w_part, preferred_element_type=jnp.float32)
+    line_rows = req_count * local_rows
+    qkv_img = qkv_img.reshape(group_count, line_rows, plane, 3, head_dim)
     log2_scale = score_scale * math.log2(math.e)
     packed = jnp.stack(
         [
@@ -207,11 +207,16 @@
         ]
     )
     packed = jnp.transpose(packed, (3, 2, 0, 1, 4)).reshape(
-        half_heads, pair_rows, 3 * group_count * head_dim
+        plane, line_rows, 3 * group_count * head_dim
     )
     by_head = lax.all_to_all(
-        packed, "tile", split_axis=0, concat_axis=0, tiled=True, axis_index_groups=same_core
-    ).reshape(seq_len, 3 * group_count * head_dim)
+        packed, "tile", split_axis=0, concat_axis=0, tiled=True, axis_index_groups=planes
+    )
+    by_head = (
+        by_head.reshape(plane, req_count, local_rows, 3 * group_count * head_dim)
+        .swapaxes(0, 1)
+        .reshape(seq_len, 3 * group_count * head_dim)
+    )
     h_txt = modulate(
         text,
         modulation[:, None, 2 * model_width : 3 * model_width],

time: 270 us -> 269 us (level)
  the two profiles are of different devices: /device:TPU:25 before, /device:TPU:9 now
where the time goes in v3:
time: 269 us; the launch traced here: 268 us
  waiting for transfers between devices  114 us (42%)
  Pallas kernels  43.8 us (16%)
  blocking collectives  32.1 us (12%)
  local copies, waits for them, and re-layouts  21.1 us (8%)
  matrix products  15.1 us (6%)
  between operations  14.4 us (5%)
  other arithmetic  14 us (5%)
  starting transfers between devices  13.7 us (5%)
    all_gather x1, waiting for transfers between devices, local(): lax.all_gather(turned, ('req', 'tile'), axis=1, tiled=True, axis_index_gr...  49.3 us
    pallas_call x1, Pallas kernels, attend_image(): pl.pallas_call(functools.partial(attend_kernel, text_len=text_len, groups...  43.8 us
    all_gather x1, blocking collectives, local(): modulation = lax.all_gather(mod_part, 'tile', axis=1, tiled=True)  32.1 us
    all_to_all x1, waiting for transfers between devices, local(): lax.all_to_all(packed, 'tile', split_axis=0, concat_axis=0, tiled=True, a...  29.3 us
    all_to_all x1, waiting for transfers between devices, local(): got = lax.all_to_all(sent, 'tile', split_axis=0, concat_axis=0, tiled=True)  16 us
    dot_general x1, matrix products, local(): jnp.einsum('gpd,dc->gpc', h_img, w_part, preferred_element_type=jnp.float32)  12.4 us
    all_gather x1, waiting for transfers between devices, local(): lax.all_gather(image, 'tile', axis=1, tiled=True, axis_index_groups=lines)  11.8 us
    ppermute x1, waiting for transfers between devices, local(): lax.ppermute(w_img, ('req', 'tile'), [(r * tile_count + x * plane + p, x...  6.93 us
  transfers between devices with their start and end apart: 5, of which 5 were waited for; matrix products, arithmetic and copies ran while one was open for 7% of the time, Pallas kernels for 0%

profile of v3, /device:TPU:9, one launch (start us, length us, event | category | flops | bytes accessed | tf_op | source)
XLA Modules:
  0.0 268.2 jit_solution(3428700511685160790)
XLA Ops:
  8.0 3.1 %collective-permute-start = (bf16[2432,48]{0,1:T(8,128)(2,1)}, bf16[2432,48]{0,1:T(8,128)(2,1)S(1)}, u32[]{:S(2)}, u32[]{:S(2)}) collective-permute-start(bf16[2432,48]{0,1:T(8,128)(2,1)} %param.20), channel_id=1, source_target_pairs={{0,0},{1,1},{2,2},{3,3},{4,4},{5,5},{6,6},{7,7},{8,32},{9,33},{10,... | collective-permute-start | bytes 700424 | tf_op jit(solution)/shard_map/ppermute | solution.py:174
  11.1 6.9 %collective-permute-done = bf16[2432,48]{0,1:T(8,128)(2,1)S(1)} collective-permute-done((bf16[2432,48]{0,1:T(8,128)(2,1)}, bf16[2432,48]{0,1:T(8,128)(2,1)S(1)}, u32[]{:S(2)}, u32[]{:S(2)}) %collective-permute-start) | collective-permute-done | bytes 233504 | tf_op jit(solution)/shard_map/ppermute | solution.py:174
  19.6 2.0 fusion.26
  21.5 32.1 %all-gather = bf16[32,304,2]{1,2,0:T(2,128)(2,1)S(1)} all-gather(bf16[1,304,2]{1,2,0:T(2,128)(2,1)S(1)} %fusion.26), channel_id=1, replica_groups=mesh['req'=4,'tile'=32] {'tile'}, dimensions={0}, use_global_device_ids=true | all-gather | bytes 40128 | tf_op jit(solution)/shard_map/all_gather | solution.py:192
  53.8 1.2 convert_reduce_fusion.1
  55.1 11.8 %all-gather.4.cloned.1.call-done = bf16[2,512,2432]{2,1,0:T(8,128)(2,1)} async-done(((bf16[2,128,2432]{2,1,0:T(8,128)(2,1)}), bf16[2,512,2432]{2,1,0:T(8,128)(2,1)}) %all-gather.4.cloned.1.call-update) | async-done | bytes 4980752 | tf_op jit(solution)/shard_map/all_gather | solution.py:173
  66.9 3.3 %convert_reduce_fusion = f32[2,512]{1,0:T(2,128)S(1)} fusion(bf16[2,512,2432]{2,1,0:T(8,128)(2,1)} %all-gather.4.cloned.1.call-done), kind=kLoop, calls=%fused_computation.1 | loop fusion | flops 4979712 | bytes 4984832 | tf_op jit(solution)/shard_map/reduce_sum | solution.py:23
  70.8 1.4 fusion.2
  72.3 49.3 %all-gather.6.cloned.1.call-done = bf16[2432,1536]{0,1:T(8,128)(2,1)} async-done(((bf16[2432,48]{0,1:T(8,128)(2,1)}), bf16[2432,1536]{0,1:T(8,128)(2,1)}) %all-gather.6.cloned.1.call-update) | async-done | bytes 7471120 | tf_op jit(solution)/shard_map/all_gather | solution.py:184
  121.6 12.4 %fusion.6 = f32[2,512,1536]{1,2,0:T(8,128)S(1)} fusion(bf16[2432,1536]{0,1:T(8,128)(2,1)} %all-gather.6.cloned.1.call-done, bf16[2,512,2432]{2,1,0:T(8,128)(2,1)} %all-gather.4.cloned.1.call-done, f32[2,2432]{1,0:T(2,128)S(1)} %get-tuple-element.23, f32[2,2432]{1,0:T(2,128)S(1)} %get-tuple-element.21, f32[2,512]{1,0:T(2,128)S(1)} %add_rsqrt_fusion.3, ...), kind=kOutput, calls=%fused_computation.8 | convolution fusion | flops 7665352704 | bytes 18790400 | tf_op jit(solution)/shard_map/gpd,dc->gpc/dot_general | solution.py:198
  134.8 1.0 fusion.20
  136.2 2.0 copy.80
  138.2 4.6 %all-to-all-start = ((bf16[8,512,384]{1,2,0:T(8,128)(2,1)}), bf16[8,512,384]{1,2,0:T(8,128)(2,1)}, u32[]{:S(2)}, u32[]{:S(2)}) async-start(bf16[8,512,384]{1,2,0:T(8,128)(2,1)} %bitcast.79), calls=%async_computation | async-start | bytes 6291456 | tf_op jit(solution)/shard_map/all_to_all | solution.py:212
  142.8 2.1 fusion.15
  145.0 3.0 %fusion.18 = bf16[2,154,2432]{2,0,1:T(2,128)(2,1)S(1)} fusion(bf16[2,154,2432]{2,0,1:T(2,128)(2,1)S(1)} %copy-done.2, f32[2,2432]{1,0:T(2,128)S(1)} %get-tuple-element.22, f32[2,2432]{1,0:T(2,128)S(1)} %get-tuple-element.20, f32[2,154]{0,1:T(8,128)S(1)} %add_rsqrt_fusion, f32[2,154]{0,1:T(8,128)S(1)} %broadcast_multiply_fusion), kind=kLoop, calls=%fused_computation.23 | loop fusion | flops 4494336 | bytes 3037600 | tf_op jit(solution)/shard_map/convert_element_type | solution.py:26
  151.1 29.3 %all-to-all-done = bf16[8,512,384]{1,2,0:T(8,128)(2,1)} async-done(((bf16[8,512,384]{1,2,0:T(8,128)(2,1)}), bf16[8,512,384]{1,2,0:T(8,128)(2,1)}, u32[]{:S(2)}, u32[]{:S(2)}) %all-to-all-start) | async-done | bytes 3145760 | tf_op jit(solution)/shard_map/all_to_all | solution.py:212
  180.5 4.6 %copy.81 = bf16[8,512,384]{2,1,0:T(8,128)(2,1)} copy(bf16[8,512,384]{1,2,0:T(8,128)(2,1)} %all-to-all-done) | data formatting | bytes 6291456 | tf_op jit(solution)/shard_map/all_to_all | solution.py:212
  185.1 4.1 %copy.82 = bf16[4,8,128,384]{3,2,1,0:T(8,128)(2,1)} copy(bf16[4,8,128,384]{3,2,0,1:T(8,128)(2,1)} %bitcast.80) | data formatting | bytes 6291456 | tf_op jit(solution)/shard_map/transpose | solution.py:217
  189.2 43.8 %shard_map.140 = (bf16[4096,128]{1,0:T(8,128)(2,1)}, bf16[256,128]{1,0:T(8,128)(2,1)}) custom-call(s32[2]{0:T(128)} %lengths_ref.1, bf16[4096,384]{1,0:T(8,128)(2,1)} %bitcast.72, bf16[4096,384]{1,0:T(8,128)(2,1)} %bitcast.73, bf16[4096,384]{1,0:T(8,128)(2,1)} %bitcast.74, bf16[256,128]{1,0:T(8,128)(2,1)} %pad.10.text_query_ref, ...), custom_call_target="tpu_custom_call" | custom-call | tf_op jit(solution)/shard_map/pallas_call | solution.py:115
  233.0 2.3 copy.92
  235.3 5.9 %all-to-all-start.1 = ((bf16[32,128,128]{1,2,0:T(8,128)(2,1)}), bf16[32,128,128]{1,2,0:T(8,128)(2,1)S(1)}, u32[]{:S(2)}, u32[]{:S(2)}) async-start(bf16[32,128,128]{1,2,0:T(8,128)(2,1)} %copy.92), calls=%async_computation.1 | async-start | bytes 2097152 | tf_op jit(solution)/shard_map/all_to_all | solution.py:248
  242.1 16.0 %all-to-all-done.1 = bf16[32,128,128]{1,2,0:T(8,128)(2,1)S(1)} async-done(((bf16[32,128,128]{1,2,0:T(8,128)(2,1)}), bf16[32,128,128]{1,2,0:T(8,128)(2,1)S(1)}, u32[]{:S(2)}, u32[]{:S(2)}) %all-to-all-start.1) | async-done | bytes 1048608 | tf_op jit(solution)/shard_map/all_to_all | solution.py:248
  258.1 1.0 copy.93
  259.1 2.3 copy.94
  (56 shorter events, 8.2 us)
Async XLA Ops:
  7.2 12.4 %copy-start = (bf16[2432,304]{0,1:T(8,128)(2,1)S(1)}, bf16[2432,304]{0,1:T(8,128)(2,1)}, u32[]{:S(2)}) copy-start(bf16[2432,304]{0,1:T(8,128)(2,1)} %param.19) | copy-start | bytes 4435972
  7.2 46.6 %copy-start.8 = (f32[64]{0:T(128)S(1)}, f32[64]{0:T(128)}, u32[]{:S(2)}) copy-start(f32[64]{0:T(128)} %param.22) | copy-start | bytes 772
  7.2 46.6 %copy-start.2 = (bf16[2,154,2432]{2,0,1:T(2,128)(2,1)S(1)}, bf16[2,154,2432]{2,0,1:T(2,128)(2,1)}, u32[]{:S(2)}) copy-start(bf16[2,154,2432]{2,0,1:T(2,128)(2,1)} %param.14) | copy-start | bytes 4494340
  7.2 59.7 %all-gather.4.cloned.1.call-start = ((), (), s32[]{:S(2)}) async-start(), calls=%async_computation.2 | async-start | bytes 6225920 | tf_op jit(solution)/shard_map/all_gather | solution.py:173
  7.9 113.6 %all-gather.6.cloned.1.call-start = ((), (), s32[]{:S(2)}) async-start(), calls=%async_computation.3 | async-start | bytes 7704576 | tf_op jit(solution)/shard_map/all_gather | solution.py:184
  8.0 10.1 %collective-permute-start = (bf16[2432,48]{0,1:T(8,128)(2,1)}, bf16[2432,48]{0,1:T(8,128)(2,1)S(1)}, u32[]{:S(2)}, u32[]{:S(2)}) collective-permute-start(bf16[2432,48]{0,1:T(8,128)(2,1)} %param.20), channel_id=1, source_target_pairs={{0,0},{1,1},{2,2},{3,3},{4,4},{5,5},{6,6},{7,7},{8,32},{9,33},{10,... | collective-permute-start | bytes 700424 | tf_op jit(solution)/shard_map/ppermute | solution.py:174
  18.1 0.7 copy-start.3
  66.9 3.9 %copy-start.1 = (bf16[2,512,2432]{2,1,0:T(8,128)(2,1)S(1)}, bf16[2,512,2432]{2,1,0:T(8,128)(2,1)}, u32[]{:S(2)}) copy-start(bf16[2,512,2432]{2,1,0:T(8,128)(2,1)} %all-gather.4.cloned.1.call-done) | copy-start | bytes 14942212
  134.0 0.8 copy-start.6
  138.2 42.3 %all-to-all-start = ((bf16[8,512,384]{1,2,0:T(8,128)(2,1)}), bf16[8,512,384]{1,2,0:T(8,128)(2,1)}, u32[]{:S(2)}, u32[]{:S(2)}) async-start(bf16[8,512,384]{1,2,0:T(8,128)(2,1)} %bitcast.79), calls=%async_computation | async-start | bytes 6291456 | tf_op jit(solution)/shard_map/all_to_all | solution.py:212
  142.8 5.2 %copy-start.7 = (bf16[2432,192]{0,1:T(8,128)(2,1)S(1)}, bf16[2432,192]{0,1:T(8,128)(2,1)}, u32[]{:S(2)}) copy-start(bf16[2432,192]{0,1:T(8,128)(2,1)} %param.21) | copy-start | bytes 2801668
  144.9 3.8 %copy-start.9 = (f32[64]{0:T(128)S(1)}, f32[64]{0:T(128)}, u32[]{:S(2)}) copy-start(f32[64]{0:T(128)} %param.24) | copy-start | bytes 772
  145.0 3.8 %copy-start.5 = (f32[64]{0:T(128)S(1)}, f32[64]{0:T(128)}, u32[]{:S(2)}) copy-start(f32[64]{0:T(128)} %param.25) | copy-start | bytes 772
  233.0 8.2 %copy-start.4 = (bf16[256,128]{1,0:T(8,128)(2,1)S(1)}, bf16[256,128]{1,0:T(8,128)(2,1)}, u32[]{:S(2)}) copy-start(bf16[256,128]{1,0:T(8,128)(2,1)} %get-tuple-element.5) | copy-start | bytes 196612
  235.3 22.8 %all-to-all-start.1 = ((bf16[32,128,128]{1,2,0:T(8,128)(2,1)}), bf16[32,128,128]{1,2,0:T(8,128)(2,1)S(1)}, u32[]{:S(2)}, u32[]{:S(2)}) async-start(bf16[32,128,128]{1,2,0:T(8,128)(2,1)} %copy.92), calls=%async_computation.1 | async-start | bytes 2097152 | tf_op jit(solution)/shard_map/all_to_all | solution.py:248
Sparse Core Ops, SparseCore 0:
  9.7 57.1 all-gather.3
  69.8 51.7 all-gather.5

commit v4 on v3

--- a/solution.py
+++ b/solution.py
@@ -165,12 +165,20 @@
     score_scale = head_dim ** (-0.5)
     req_count = lax.axis_size("req")
     plane = tile_count // req_count
-    lines = [[x * plane + p for x in range(req_count)] for p in range(plane)]
     planes = [[x * plane + p for p in range(plane)] for x in range(req_count)]
     all_planes = [
         [r * tile_count + t for r in range(req_count) for t in planes[x]] for x in range(req_count)
     ]
-    image = lax.all_gather(image, "tile", axis=1, tiled=True, axis_index_groups=lines)
+    ahead = [(t, (t + plane) % tile_count) for t in range(tile_count)]
+    back = [(to, at) for at, to in ahead]
+    from_last = lax.ppermute(image, "tile", ahead)
+    from_next = lax.ppermute(image, "tile", back)
+    half_group = group_count // 2
+    far_low = lax.ppermute(from_next[:half_group], "tile", back)
+    far_high = lax.ppermute(from_last[half_group:], "tile", ahead)
+    image = jnp.concatenate(
+        [image, from_next, jnp.concatenate([far_low, far_high], axis=0), from_last], axis=1
+    )
     turned = lax.ppermute(
         w_img,
         ("req", "tile"),
@@ -213,10 +221,12 @@
         packed, "tile", split_axis=0, concat_axis=0, tiled=True, axis_index_groups=planes
     )
     by_head = (
-        by_head.reshape(plane, req_count, local_rows, 3 * group_count * head_dim)
-        .swapaxes(0, 1)
-        .reshape(seq_len, 3 * group_count * head_dim)
-    )
+        jnp.roll(
+            by_head.reshape(plane, req_count, local_rows, 3 * group_count * head_dim).swapaxes(0, 1),
+            lax.axis_index("tile") // plane,
+            axis=0,
+        )
+    ).reshape(seq_len, 3 * group_count * head_dim)
     h_txt = modulate(
         text,
         modulation[:, None, 2 * model_width : 3 * model_width],

time: 269 us -> 259 us (0.963)
  the two profiles are of different devices: /device:TPU:9 before, /device:TPU:25 now
where the time goes in v4:
time: 259 us; the launch traced here: 257 us
  waiting for transfers between devices  74.2 us (29%)
  Pallas kernels  49.1 us (19%)
  blocking collectives  46.1 us (18%)
  local copies, waits for them, and re-layouts  22.9 us (9%)
  starting transfers between devices  17.6 us (7%)
  other arithmetic  17.3 us (7%)
  matrix products  15.1 us (6%)
  between operations  14.4 us (6%)
    pallas_call x1, Pallas kernels, attend_image(): pl.pallas_call(functools.partial(attend_kernel, text_len=text_len, groups...  49.1 us
    all_gather x1, blocking collectives, local(): modulation = lax.all_gather(mod_part, 'tile', axis=1, tiled=True)  46.1 us
    all_to_all x1, waiting for transfers between devices, local(): lax.all_to_all(packed, 'tile', split_axis=0, concat_axis=0, tiled=True, a...  29.4 us
    all_to_all x1, waiting for transfers between devices, local(): got = lax.all_to_all(sent, 'tile', split_axis=0, concat_axis=0, tiled=True)  16.1 us
    ppermute x1, waiting for transfers between devices, local(): lax.ppermute(w_img, ('req', 'tile'), [(r * tile_count + x * plane + p, x...  13.5 us
    ppermute x1, waiting for transfers between devices, local(): far_low = lax.ppermute(from_next[:half_group], 'tile', back)  12.6 us
    dot_general x1, matrix products, local(): jnp.einsum('gpd,dc->gpc', h_img, w_part, preferred_element_type=jnp.float32)  12.5 us
    unnamed x25, local copies, waits for them, and re-layouts  6.08 us
  transfers between devices with their start and end apart: 8, of which 5 were waited for; matrix products, arithmetic and copies ran while one was open for 8% of the time, Pallas kernels for 0%

profile of v4, /device:TPU:25, one launch (start us, length us, event | category | flops | bytes accessed | tf_op | source)
XLA Modules:
  0.0 256.8 jit_solution(10689281340658488298)
XLA Ops:
  7.2 4.3 %collective-permute-start.4 = (bf16[2432,48]{0,1:T(8,128)(2,1)}, bf16[2432,48]{0,1:T(8,128)(2,1)S(1)}, u32[]{:S(2)}, u32[]{:S(2)}) collective-permute-start(bf16[2432,48]{0,1:T(8,128)(2,1)} %param.20), channel_id=1, source_target_pairs={{0,0},{1,1},{2,2},{3,3},{4,4},{5,5},{6,6},{7,7},{8,32},{9,33},{10,... | collective-permute-start | bytes 700424 | tf_op jit(solution)/shard_map/ppermute | solution.py:182
  11.6 13.5 %collective-permute-done.4 = bf16[2432,48]{0,1:T(8,128)(2,1)S(1)} collective-permute-done((bf16[2432,48]{0,1:T(8,128)(2,1)}, bf16[2432,48]{0,1:T(8,128)(2,1)S(1)}, u32[]{:S(2)}, u32[]{:S(2)}) %collective-permute-start.4) | collective-permute-done | bytes 233504 | tf_op jit(solution)/shard_map/ppermute | solution.py:182
  25.9 1.4 collective-permute-start.2
  28.1 2.0 fusion.27
  30.1 46.1 %all-gather = bf16[32,304,2]{1,2,0:T(2,128)(2,1)S(1)} all-gather(bf16[1,304,2]{1,2,0:T(2,128)(2,1)S(1)} %fusion.27), channel_id=1, replica_groups=mesh['req'=4,'tile'=32] {'tile'}, dimensions={0}, use_global_device_ids=true | all-gather | bytes 40128 | tf_op jit(solution)/shard_map/all_gather | solution.py:200
  80.2 1.5 collective-permute-start.3
  81.7 12.6 %collective-permute-done.1 = bf16[1,128,2432]{2,1,0:T(8,128)(2,1)S(1)} collective-permute-done((bf16[1,128,2432]{2,1,0:T(8,128)(2,1)S(1)}, bf16[1,128,2432]{2,1,0:T(8,128)(2,1)S(1)}, u32[]{:S(2)}, u32[]{:S(2)}) %collective-permute-start.1) | collective-permute-done | bytes 622624 | tf_op jit(solution)/shard_map/ppermute | solution.py:177
  94.3 2.6 %collective-permute-done.3 = bf16[1,128,2432]{2,1,0:T(8,128)(2,1)S(1)} collective-permute-done((bf16[1,128,2432]{2,1,0:T(8,128)(2,1)S(1)}, bf16[1,128,2432]{2,1,0:T(8,128)(2,1)S(1)}, u32[]{:S(2)}, u32[]{:S(2)}) %collective-permute-start.3) | collective-permute-done | bytes 622624 | tf_op jit(solution)/shard_map/ppermute | solution.py:178
  96.9 3.4 %convert_reduce_fusion = (f32[2,512]{1,0:T(2,128)S(1)}, bf16[2,512,2432]{2,1,0:T(8,128)(2,1)S(1)}) fusion(bf16[2,128,2432]{2,1,0:T(8,128)(2,1)} %collective-permute-done.2, bf16[1,128,2432]{2,1,0:T(8,128)(2,1)S(1)} %collective-permute-done.3, bf16[1,128,2432]{2,1,0:T(8,128)(2,1)S(1)} %collective-permute-done.1, ...), kind=kLoop, calls=%fused_computation.1 | loop fusion | flops 29883392 | bytes 9965568 | tf_op jit(solution)/shard_map/reduce_sum | solution.py:23
  100.4 2.2 copy-done.1
  104.1 12.5 %fusion.6 = f32[2,512,1536]{1,2,0:T(8,128)S(1)} fusion(bf16[2432,1536]{0,1:T(8,128)(2,1)} %all-gather.3.cloned.1.call-done, bf16[2,512,2432]{2,1,0:T(8,128)(2,1)} %copy-done.1, f32[2,2432]{1,0:T(2,128)S(1)} %get-tuple-element.25, f32[2,2432]{1,0:T(2,128)S(1)} %get-tuple-element.23, f32[2,512]{1,0:T(2,128)S(1)} %add_rsqrt_fusion.3, ...), kind=kOutput, calls=%fused_computation.8 | convolution fusion | flops 7665352704 | bytes 18790400 | tf_op jit(solution)/shard_map/gpd,dc->gpc/dot_general | solution.py:206
  118.7 2.0 copy.80
  120.7 5.5 %all-to-all-start = ((bf16[8,512,384]{1,2,0:T(8,128)(2,1)}), bf16[8,512,384]{1,2,0:T(8,128)(2,1)}, u32[]{:S(2)}, u32[]{:S(2)}) async-start(bf16[8,512,384]{1,2,0:T(8,128)(2,1)} %bitcast.79), calls=%async_computation | async-start | bytes 6291456 | tf_op jit(solution)/shard_map/all_to_all | solution.py:220
  126.2 2.1 fusion.16
  128.4 3.0 %fusion.19 = bf16[2,154,2432]{2,0,1:T(2,128)(2,1)S(1)} fusion(bf16[2,154,2432]{2,0,1:T(2,128)(2,1)S(1)} %copy-done.2, f32[2,2432]{1,0:T(2,128)S(1)} %get-tuple-element.24, f32[2,2432]{1,0:T(2,128)S(1)} %get-tuple-element.22, f32[2,154]{0,1:T(8,128)S(1)} %add_rsqrt_fusion, f32[2,154]{0,1:T(8,128)S(1)} %broadcast_multiply_fusion), kind=kLoop, calls=%fused_computation.27 | loop fusion | flops 4494336 | bytes 3037600 | tf_op jit(solution)/shard_map/convert_element_type | solution.py:26
  134.5 29.4 %all-to-all-done = bf16[8,512,384]{1,2,0:T(8,128)(2,1)} async-done(((bf16[8,512,384]{1,2,0:T(8,128)(2,1)}), bf16[8,512,384]{1,2,0:T(8,128)(2,1)}, u32[]{:S(2)}, u32[]{:S(2)}) %all-to-all-start) | async-done | bytes 3145760 | tf_op jit(solution)/shard_map/all_to_all | solution.py:220
  163.9 4.6 %copy.81 = bf16[8,512,384]{2,1,0:T(8,128)(2,1)} copy(bf16[8,512,384]{1,2,0:T(8,128)(2,1)} %all-to-all-done) | data formatting | bytes 6291456 | tf_op jit(solution)/shard_map/all_to_all | solution.py:220
  168.5 3.2 %fusion.13 = bf16[4,8,128,384]{3,2,0,1:T(8,128)(2,1)S(1)} fusion(s32[]{:T(128)S(6)} %select_n.19, bf16[4,8,128,384]{3,2,0,1:T(8,128)(2,1)} %bitcast.80), kind=kLoop, calls=%fused_computation.20 | loop fusion | flops 1572864 | bytes 6291460 | tf_op jit(solution)/shard_map/jit(_roll_dynamic)/concatenate | solution.py:224
  171.7 2.0 copy.82
  173.8 49.1 %shard_map.140 = (bf16[4096,128]{1,0:T(8,128)(2,1)}, bf16[256,128]{1,0:T(8,128)(2,1)}) custom-call(s32[2]{0:T(128)} %lengths_ref.1, bf16[4096,384]{1,0:T(8,128)(2,1)} %bitcast.72, bf16[4096,384]{1,0:T(8,128)(2,1)} %bitcast.73, bf16[4096,384]{1,0:T(8,128)(2,1)} %bitcast.74, bf16[256,128]{1,0:T(8,128)(2,1)} %pad.10.text_query_ref, ...), custom_call_target="tpu_custom_call" | custom-call | tf_op jit(solution)/shard_map/pallas_call | solution.py:115
  222.9 2.3 copy.92
  225.2 4.5 %all-to-all-start.1 = ((bf16[32,128,128]{1,2,0:T(8,128)(2,1)}), bf16[32,128,128]{1,2,0:T(8,128)(2,1)S(1)}, u32[]{:S(2)}, u32[]{:S(2)}) async-start(bf16[32,128,128]{1,2,0:T(8,128)(2,1)} %copy.92), calls=%async_computation.1 | async-start | bytes 2097152 | tf_op jit(solution)/shard_map/all_to_all | solution.py:258
  230.6 16.1 %all-to-all-done.1 = bf16[32,128,128]{1,2,0:T(8,128)(2,1)S(1)} async-done(((bf16[32,128,128]{1,2,0:T(8,128)(2,1)}), bf16[32,128,128]{1,2,0:T(8,128)(2,1)S(1)}, u32[]{:S(2)}, u32[]{:S(2)}) %all-to-all-start.1) | async-done | bytes 1048608 | tf_op jit(solution)/shard_map/all_to_all | solution.py:258
  247.7 2.3 copy.94
  (66 shorter events, 14.2 us)
Async XLA Ops:
  7.2 20.9 %copy-start = (bf16[2432,304]{0,1:T(8,128)(2,1)S(1)}, bf16[2432,304]{0,1:T(8,128)(2,1)}, u32[]{:S(2)}) copy-start(bf16[2432,304]{0,1:T(8,128)(2,1)} %param.19) | copy-start | bytes 4435972
  7.2 69.2 %copy-start.9 = (f32[64]{0:T(128)S(1)}, f32[64]{0:T(128)}, u32[]{:S(2)}) copy-start(f32[64]{0:T(128)} %param.22) | copy-start | bytes 772
  7.2 69.2 %copy-start.2 = (bf16[2,154,2432]{2,0,1:T(2,128)(2,1)S(1)}, bf16[2,154,2432]{2,0,1:T(2,128)(2,1)}, u32[]{:S(2)}) copy-start(bf16[2,154,2432]{2,0,1:T(2,128)(2,1)} %param.14) | copy-start | bytes 4494340
  7.2 96.9 %all-gather.3.cloned.1.call-start = ((), (), s32[]{:S(2)}) async-start(), calls=%async_computation.2 | async-start | bytes 7704576 | tf_op jit(solution)/shard_map/all_gather | solution.py:192
  7.2 17.8 %collective-permute-start.4 = (bf16[2432,48]{0,1:T(8,128)(2,1)}, bf16[2432,48]{0,1:T(8,128)(2,1)S(1)}, u32[]{:S(2)}, u32[]{:S(2)}) collective-permute-start(bf16[2432,48]{0,1:T(8,128)(2,1)} %param.20), channel_id=1, source_target_pairs={{0,0},{1,1},{2,2},{3,3},{4,4},{5,5},{6,6},{7,7},{8,32},{9,33},{10,... | collective-permute-start | bytes 700424 | tf_op jit(solution)/shard_map/ppermute | solution.py:182
  25.1 0.7 copy-start.4
  25.8 51.9 %collective-permute-start = (bf16[2,128,2432]{2,1,0:T(8,128)(2,1)}, bf16[2,128,2432]{2,1,0:T(8,128)(2,1)}, u32[]{:S(2)}, u32[]{:S(2)}) collective-permute-start(bf16[2,128,2432]{2,1,0:T(8,128)(2,1)} %param.13), channel_id=1, source_target_pairs={{8,0},{9,1},{10,2},{11,3},{12,4},{13,5},{14,6},{15,7},{16,8},{17,9... | collective-permute-start | bytes 3735560 | tf_op jit(solution)/shard_map/ppermute | solution.py:175
  25.9 53.3 %collective-permute-start.2 = (bf16[2,128,2432]{2,1,0:T(8,128)(2,1)}, bf16[2,128,2432]{2,1,0:T(8,128)(2,1)}, u32[]{:S(2)}, u32[]{:S(2)}) collective-permute-start(bf16[2,128,2432]{2,1,0:T(8,128)(2,1)} %param.13), channel_id=1, source_target_pairs={{0,8},{1,9},{2,10},{3,11},{4,12},{5,13},{6,14},{7,15},{8,16},{9,17... | collective-permute-start | bytes 3735560 | tf_op jit(solution)/shard_map/ppermute | solution.py:174
  76.4 20.6 %copy-start.3 = (bf16[2,128,2432]{2,1,0:T(8,128)(2,1)S(1)}, bf16[2,128,2432]{2,1,0:T(8,128)(2,1)}, u32[]{:S(2)}) copy-start(bf16[2,128,2432]{2,1,0:T(8,128)(2,1)} %param.13) | copy-start | bytes 3735556
  78.8 15.5 %collective-permute-start.1 = (bf16[1,128,2432]{2,1,0:T(8,128)(2,1)S(1)}, bf16[1,128,2432]{2,1,0:T(8,128)(2,1)S(1)}, u32[]{:S(2)}, u32[]{:S(2)}) collective-permute-start(bf16[1,128,2432]{2,1,0:T(8,128)(2,1)S(1)} %slice.54), channel_id=1, source_target_pairs={{8,0},{9,1},{10,2},{11,3},{12,4},{13,5},{14,6},{15,7},{16,8},{17,9... | collective-permute-start | bytes 1867784 | tf_op jit(solution)/shard_map/ppermute | solution.py:177
  80.2 16.7 %collective-permute-start.3 = (bf16[1,128,2432]{2,1,0:T(8,128)(2,1)S(1)}, bf16[1,128,2432]{2,1,0:T(8,128)(2,1)S(1)}, u32[]{:S(2)}, u32[]{:S(2)}) collective-permute-start(bf16[1,128,2432]{2,1,0:T(8,128)(2,1)S(1)} %slice.55), channel_id=1, source_target_pairs={{0,8},{1,9},{2,10},{3,11},{4,12},{5,13},{6,14},{7,15},{8,16},{9,17... | collective-permute-start | bytes 1867784 | tf_op jit(solution)/shard_map/ppermute | solution.py:178
  100.4 2.2 copy-start.1
  116.5 0.8 copy-start.7
  120.7 43.2 %all-to-all-start = ((bf16[8,512,384]{1,2,0:T(8,128)(2,1)}), bf16[8,512,384]{1,2,0:T(8,128)(2,1)}, u32[]{:S(2)}, u32[]{:S(2)}) async-start(bf16[8,512,384]{1,2,0:T(8,128)(2,1)} %bitcast.79), calls=%async_computation | async-start | bytes 6291456 | tf_op jit(solution)/shard_map/all_to_all | solution.py:220
  126.2 5.1 %copy-start.8 = (bf16[2432,192]{0,1:T(8,128)(2,1)S(1)}, bf16[2432,192]{0,1:T(8,128)(2,1)}, u32[]{:S(2)}) copy-start(bf16[2432,192]{0,1:T(8,128)(2,1)} %param.21) | copy-start | bytes 2801668
  128.4 3.8 %copy-start.10 = (f32[64]{0:T(128)S(1)}, f32[64]{0:T(128)}, u32[]{:S(2)}) copy-start(f32[64]{0:T(128)} %param.24) | copy-start | bytes 772
  128.4 3.8 %copy-start.6 = (f32[64]{0:T(128)S(1)}, f32[64]{0:T(128)}, u32[]{:S(2)}) copy-start(f32[64]{0:T(128)} %param.25) | copy-start | bytes 772
  222.9 6.8 %copy-start.5 = (bf16[256,128]{1,0:T(8,128)(2,1)S(1)}, bf16[256,128]{1,0:T(8,128)(2,1)}, u32[]{:S(2)}) copy-start(bf16[256,128]{1,0:T(8,128)(2,1)} %get-tuple-element.5) | copy-start | bytes 196612
  225.2 21.5 %all-to-all-start.1 = ((bf16[32,128,128]{1,2,0:T(8,128)(2,1)}), bf16[32,128,128]{1,2,0:T(8,128)(2,1)S(1)}, u32[]{:S(2)}, u32[]{:S(2)}) async-start(bf16[32,128,128]{1,2,0:T(8,128)(2,1)} %copy.92), calls=%async_computation.1 | async-start | bytes 2097152 | tf_op jit(solution)/shard_map/all_to_all | solution.py:258
Sparse Core Ops, SparseCore 0:
  25.9 51.3 all-gather.2
